TPU v7x, 32 devices: a whole 2x2x4 slice. The times are simulated.
32 devices in a mesh: ctx: 8 (over y, x, core), wsh: 4 (over z).
Axes of the slice: x: 2, y: 2, z: 4, core: 2. Of those that a mesh axis runs over, the one named last changes fastest.
Arguments:
- layer_input: bfloat16 [4, 1024, 960], P('wsh', 'ctx'), may hold values from -50 to 50
- positions: int32 [1024], replicated, may hold values from 0 to 1023, as said below
- first_gain: bfloat16 [960], P('wsh'), may hold values from 0.5 to 2
- query_weight: bfloat16 [960, 960], P('wsh'), may hold values from -1 to 1
- key_weight: bfloat16 [960, 320], P('wsh'), may hold values from -1 to 1
- value_proj_weight: bfloat16 [960, 320], P('wsh'), may hold values from -0.1875 to 0.1875
- output_weight: bfloat16 [960, 960], P('wsh'), may hold values from -1.5 to 1.5
- second_gain: bfloat16 [960], P('wsh'), may hold values from 0.5 to 2
- gate_weight: bfloat16 [960, 2560], P('wsh'), may hold values from -0.1875 to 0.1875
- up_weight: bfloat16 [960, 2560], P('wsh'), may hold values from -0.1875 to 0.1875
- down_weight: bfloat16 [2560, 960], P('wsh'), may hold values from -0.125 to 0.125
- cotangent: bfloat16 [4, 1024, 960], P('wsh', 'ctx'), may hold values from -6 to 6
Outputs:
- layer_output: bfloat16 [4, 1024, 960], P('wsh', 'ctx')
- input_gradient: float32 [4, 1024, 960], P('wsh', 'ctx')
- first_gain_gradient: float32 [960], P('wsh')
- query_weight_gradient: float32 [960, 960], P('wsh')
- key_weight_gradient: float32 [960, 320], P('wsh')
- value_weight_gradient: float32 [960, 320], P('wsh')
- output_weight_gradient: float32 [960, 960], P('wsh')
- second_gain_gradient: float32 [960], P('wsh')
- gate_weight_gradient: float32 [960, 2560], P('wsh')
- up_weight_gradient: float32 [960, 2560], P('wsh')
- down_weight_gradient: float32 [2560, 960], P('wsh')
Inputs may be any that keep to these rules, and one draw needn't show every extreme that they name: Along ctx, device c holds two blocks of 64 consecutive positions, each starting at a multiple of 64: first block b_c, then block 15 - b_c; the b_c run over 0 to 7, each once.
All inputs are finite; a program needn't handle non-finite values.
Results may differ from a plain program's by a relative error of at most 0.023.
The roundings to bfloat16 on the way count: a program that leaves them out, or rounds other values in their place, can miss the bound.
Values may be sent and summed in bfloat16 or wider, within the bound.
A program may use at most 192 MiB of HBM per device.

v0:
```python
import math

import jax
import jax.numpy as jnp
from jax import lax
from jax.sharding import PartitionSpec as P

QUERY_HEADS = 15
KEY_VALUE_HEADS = 5
HEAD_SIZE = 64


EPS = 1e-05
ROPE_BASE = 10000.0
NEG_FILL = -1e30


def matrix_product(left, right):
    return jnp.dot(left, right, preferred_element_type=jnp.float32)


def times_transposed(left, right):
    return lax.dot_general(
        left, right, (((1,), (1,)), ((), ())), preferred_element_type=jnp.float32
    )


def token_sum(left, right):
    return lax.dot_general(
        left, right, (((0,), (0,)), ((), ())), preferred_element_type=jnp.float32
    )


def norm_scale(inputs):
    return lax.rsqrt(jnp.mean(inputs * inputs, axis=-1, keepdims=True) + EPS)


def norm_back(incoming, normed, scale, gain):
    scaled = incoming * gain
    return scale * (scaled - normed * jnp.mean(scaled * normed, axis=-1, keepdims=True))


def rope_tables(places, head_width):
    half = head_width // 2
    frequency = ROPE_BASE ** (-2.0 * jnp.arange(half, dtype=jnp.float32) / head_width)
    angle = places.astype(jnp.float32)[:, None] * frequency[None, :]
    return (jnp.cos(angle)[:, None, :], jnp.sin(angle)[:, None, :])


def apply_rotary(inputs, cosine_table, sine_table):
    half = inputs.shape[-1] // 2
    first = inputs[..., :half]
    second = inputs[..., half:]
    return jnp.concatenate(
        [first * cosine_table - second * sine_table, second * cosine_table + first * sine_table],
        axis=-1,
    )


def apply_rotary_back(incoming, cosine_table, sine_table):
    half = incoming.shape[-1] // 2
    first = incoming[..., :half]
    second = incoming[..., half:]
    return jnp.concatenate(
        [first * cosine_table + second * sine_table, second * cosine_table - first * sine_table],
        axis=-1,
    )


def attend_forward(
    query_rows_local,
    query_places,
    keys_rotated_pos,
    value_rows_local,
    key_places,
    tiles,
    tile_piece,
    score_scale,
):
    query_rows, head_groups, repeats, head_width = query_rows_local.shape

    def visit(index, carry):
        running, totals, weighted = carry
        begin = index * tile_piece
        key_tile = lax.dynamic_slice_in_dim(keys_rotated_pos, begin, tile_piece, 0)
        value_tile = lax.dynamic_slice_in_dim(value_rows_local, begin, tile_piece, 0)
        place_tile = lax.dynamic_slice_in_dim(key_places, begin, tile_piece, 0)
        scores = (
            jnp.einsum(
                "qgrd,kgd->qgrk", query_rows_local, key_tile, preferred_element_type=jnp.float32
            )
            * score_scale
        )
        allowed = (place_tile[None, :] <= query_places[:, None])[:, None, None, :]
        scores = jnp.where(allowed, scores, NEG_FILL)
        newest = jnp.maximum(running, jnp.max(scores, axis=-1))
        factor = jnp.exp(running - newest)
        portion = jnp.exp(scores - newest[..., None])
        totals = totals * factor + jnp.sum(portion, axis=-1)
        weighted = weighted * factor[..., None] + jnp.einsum(
            "qgrk,kgd->qgrd",
            portion.astype(jnp.bfloat16),
            value_tile,
            preferred_element_type=jnp.float32,
        )
        return (newest, totals, weighted)

    start_state = (
        jnp.full((query_rows, head_groups, repeats), NEG_FILL, jnp.float32),
        jnp.zeros((query_rows, head_groups, repeats), jnp.float32),
        jnp.zeros((query_rows, head_groups, repeats, head_width), jnp.float32),
    )
    running, totals, weighted = lax.fori_loop(0, tiles, visit, start_state)
    return ((weighted / totals[..., None]).astype(jnp.bfloat16), running + jnp.log(totals))


def attend_backward(
    query_rows_local,
    query_places,
    attention_result_back,
    log_total,
    delta_rows,
    keys_rotated_pos,
    value_rows_local,
    key_places,
    tiles,
    tile_piece,
    score_scale,
    keys_gradient_back,
    values_gradient_back,
):

    def visit(index, carry):
        query_gradient_back, keys_gradient_back, values_gradient_back = carry
        begin = index * tile_piece
        key_tile = lax.dynamic_slice_in_dim(keys_rotated_pos, begin, tile_piece, 0)
        value_tile = lax.dynamic_slice_in_dim(value_rows_local, begin, tile_piece, 0)
        place_tile = lax.dynamic_slice_in_dim(key_places, begin, tile_piece, 0)
        scores = (
            jnp.einsum(
                "qgrd,kgd->qgrk", query_rows_local, key_tile, preferred_element_type=jnp.float32
            )
            * score_scale
        )
        allowed = (place_tile[None, :] <= query_places[:, None])[:, None, None, :]
        scores = jnp.where(allowed, scores, NEG_FILL)
        probability = jnp.exp(scores - log_total[..., None])
        value_dots = jnp.einsum(
            "qgrd,kgd->qgrk", attention_result_back, value_tile, preferred_element_type=jnp.float32
        )
        score_grad = (probability * (value_dots - delta_rows[..., None]) * score_scale).astype(
            jnp.bfloat16
        )
        query_gradient_back = query_gradient_back + jnp.einsum(
            "qgrk,kgd->qgrd", score_grad, key_tile, preferred_element_type=jnp.float32
        )
        key_part = jnp.einsum(
            "qgrk,qgrd->kgd", score_grad, query_rows_local, preferred_element_type=jnp.float32
        )
        value_part = jnp.einsum(
            "qgrk,qgrd->kgd",
            probability.astype(jnp.bfloat16),
            attention_result_back,
            preferred_element_type=jnp.float32,
        )
        keys_gradient_back = lax.dynamic_update_slice_in_dim(
            keys_gradient_back,
            lax.dynamic_slice_in_dim(keys_gradient_back, begin, tile_piece, 0) + key_part,
            begin,
            0,
        )
        values_gradient_back = lax.dynamic_update_slice_in_dim(
            values_gradient_back,
            lax.dynamic_slice_in_dim(values_gradient_back, begin, tile_piece, 0) + value_part,
            begin,
            0,
        )
        return (query_gradient_back, keys_gradient_back, values_gradient_back)

    start_state = (
        jnp.zeros(query_rows_local.shape, jnp.float32),
        keys_gradient_back,
        values_gradient_back,
    )
    return lax.fori_loop(0, tiles, visit, start_state)


def per_device(
    layer_input,
    positions,
    first_gain,
    query_weight,
    key_weight,
    value_proj_weight,
    output_weight,
    second_gain,
    gate_weight,
    up_weight,
    down_weight,
    cotangent,
):
    shards = (
        first_gain,
        query_weight,
        key_weight,
        value_proj_weight,
        output_weight,
        second_gain,
        gate_weight,
        up_weight,
        down_weight,
    )
    gathered = (
        lax.all_gather(shards[0], "wsh", axis=0, tiled=True),
        lax.all_gather(shards[1], "wsh", axis=0, tiled=True),
        lax.all_gather(shards[2], "wsh", axis=0, tiled=True),
        lax.all_gather(shards[3], "wsh", axis=0, tiled=True),
        lax.all_gather(shards[4], "wsh", axis=0, tiled=True),
        lax.all_gather(shards[5], "wsh", axis=0, tiled=True),
        lax.all_gather(shards[6], "wsh", axis=0, tiled=True),
        lax.all_gather(shards[7], "wsh", axis=0, tiled=True),
        lax.all_gather(shards[8], "wsh", axis=0, tiled=True),
    )
    (
        first_scale,
        query_matrix,
        key_projection,
        value_projection,
        output_matrix,
        second_scale,
        gate_matrix,
        up_matrix,
        down_matrix,
    ) = gathered
    tokens = layer_input[0]
    incoming_rows = cotangent[0]
    worker_rows = tokens.shape[0]
    half_rows = worker_rows // 2
    tile_piece = 2 * worker_rows
    sequence_rows = positions.shape[0]
    head_groups = QUERY_HEADS // KEY_VALUE_HEADS
    score_scale = 1.0 / math.sqrt(HEAD_SIZE)
    own_places = lax.dynamic_slice_in_dim(
        positions, lax.axis_index("ctx") * worker_rows, worker_rows, 0
    )
    cosine_table, sine_table = rope_tables(own_places, HEAD_SIZE)
    inputs = tokens.astype(jnp.float32)
    scale_one = norm_scale(inputs)
    normed_one = inputs * scale_one
    hidden_first = (normed_one * first_scale.astype(jnp.float32)).astype(jnp.bfloat16)
    query_rows_local = apply_rotary(
        matrix_product(hidden_first, query_matrix).reshape(worker_rows, QUERY_HEADS, HEAD_SIZE),
        cosine_table,
        sine_table,
    ).astype(jnp.bfloat16)
    keys_rotated_pos = apply_rotary(
        matrix_product(hidden_first, key_projection).reshape(
            worker_rows, KEY_VALUE_HEADS, HEAD_SIZE
        ),
        cosine_table,
        sine_table,
    ).astype(jnp.bfloat16)
    value_rows_local = matrix_product(hidden_first, value_projection).astype(jnp.bfloat16)
    keys_gathered_full, values_gathered_full = (
        lax.all_gather(
            keys_rotated_pos.reshape(worker_rows, KEY_VALUE_HEADS * HEAD_SIZE),
            "ctx",
            axis=0,
            tiled=True,
        ),
        lax.all_gather(value_rows_local, "ctx", axis=0, tiled=True),
    )
    block_count = sequence_rows // half_rows
    block_ids = positions.reshape(block_count, half_rows)[:, 0] // half_rows
    slots = jnp.arange(block_count, dtype=jnp.int32)
    source = jnp.sum(jnp.where(block_ids[None, :] == slots[:, None], slots[None, :], 0), axis=1)

    def ordered_blocks(array):
        return jnp.take(
            array.reshape((block_count, half_rows) + array.shape[1:]), source, axis=0
        ).reshape(array.shape)

    def blocks_per_worker(array):
        return jnp.take(
            array.reshape((block_count, half_rows) + array.shape[1:]), block_ids, axis=0
        ).reshape(array.shape)

    keys_ordered = ordered_blocks(keys_gathered_full).reshape(
        sequence_rows, KEY_VALUE_HEADS, HEAD_SIZE
    )
    values_ordered = ordered_blocks(values_gathered_full).reshape(
        sequence_rows, KEY_VALUE_HEADS, HEAD_SIZE
    )
    places_sorted = ordered_blocks(positions)
    query_head_groups = query_rows_local.reshape(
        worker_rows, KEY_VALUE_HEADS, head_groups, HEAD_SIZE
    )
    attended_parts = []
    log_parts = []
    tile_counts = []
    for half_index in range(2):
        lower = half_index * half_rows
        place_half = own_places[lower : lower + half_rows]
        needed = (jnp.max(place_half) + tile_piece) // tile_piece
        tile_counts.append(needed)
        attended_half, log_half = attend_forward(
            query_head_groups[lower : lower + half_rows],
            place_half,
            keys_ordered,
            values_ordered,
            places_sorted,
            needed,
            tile_piece,
            score_scale,
        )
        attended_parts.append(attended_half)
        log_parts.append(log_half)
    attention_result = jnp.concatenate(attended_parts, axis=0).reshape(
        worker_rows, QUERY_HEADS * HEAD_SIZE
    )
    mixed = inputs + matrix_product(attention_result, output_matrix)
    scale_two = norm_scale(mixed)
    normed_two = mixed * scale_two
    hidden_two = (normed_two * second_scale.astype(jnp.float32)).astype(jnp.bfloat16)
    gate = matrix_product(hidden_two, gate_matrix)
    upward = matrix_product(hidden_two, up_matrix)
    sigma = jax.nn.sigmoid(gate)
    activated = (gate * sigma * upward).astype(jnp.bfloat16)
    layer_output = (mixed + matrix_product(activated, down_matrix)).astype(jnp.bfloat16)
    activated_back = times_transposed(incoming_rows, down_matrix)
    gate_back = (activated_back * upward * sigma * (1.0 + gate * (1.0 - sigma))).astype(
        jnp.bfloat16
    )
    up_back = (activated_back * gate * sigma).astype(jnp.bfloat16)
    second_back = times_transposed(gate_back, gate_matrix) + times_transposed(up_back, up_matrix)
    second_gradient = jnp.sum(second_back * normed_two, axis=0)
    mixed_back = incoming_rows.astype(jnp.float32) + norm_back(
        second_back, normed_two, scale_two, second_scale.astype(jnp.float32)
    )
    mixed_low = mixed_back.astype(jnp.bfloat16)
    attention_result_back = times_transposed(mixed_low, output_matrix).astype(jnp.bfloat16)
    backward_groups = attention_result_back.reshape(
        worker_rows, KEY_VALUE_HEADS, head_groups, HEAD_SIZE
    )
    delta_rows = jnp.sum(
        backward_groups.astype(jnp.float32)
        * attention_result.reshape(worker_rows, KEY_VALUE_HEADS, head_groups, HEAD_SIZE).astype(
            jnp.float32
        ),
        axis=-1,
    )
    keys_gradient_back = jnp.zeros((sequence_rows, KEY_VALUE_HEADS, HEAD_SIZE), jnp.float32)
    values_gradient_back = jnp.zeros((sequence_rows, KEY_VALUE_HEADS, HEAD_SIZE), jnp.float32)
    query_parts = []
    for half_index in range(2):
        lower = half_index * half_rows
        query_half, keys_gradient_back, values_gradient_back = attend_backward(
            query_head_groups[lower : lower + half_rows],
            own_places[lower : lower + half_rows],
            backward_groups[lower : lower + half_rows],
            log_parts[half_index],
            delta_rows[lower : lower + half_rows],
            keys_ordered,
            values_ordered,
            places_sorted,
            tile_counts[half_index],
            tile_piece,
            score_scale,
            keys_gradient_back,
            values_gradient_back,
        )
        query_parts.append(query_half)
    query_gradient_back = jnp.concatenate(query_parts, axis=0).reshape(
        worker_rows, QUERY_HEADS, HEAD_SIZE
    )
    key_portion_local, value_share = (
        lax.psum_scatter(
            blocks_per_worker(keys_gradient_back).reshape(
                sequence_rows, KEY_VALUE_HEADS * HEAD_SIZE
            ),
            "ctx",
            scatter_dimension=0,
            tiled=True,
        ),
        lax.psum_scatter(
            blocks_per_worker(values_gradient_back).reshape(
                sequence_rows, KEY_VALUE_HEADS * HEAD_SIZE
            ),
            "ctx",
            scatter_dimension=0,
            tiled=True,
        ),
    )
    query_rounded = (
        apply_rotary_back(query_gradient_back, cosine_table, sine_table)
        .reshape(worker_rows, QUERY_HEADS * HEAD_SIZE)
        .astype(jnp.bfloat16)
    )
    key_lowered = (
        apply_rotary_back(
            key_portion_local.reshape(worker_rows, KEY_VALUE_HEADS, HEAD_SIZE),
            cosine_table,
            sine_table,
        )
        .reshape(worker_rows, KEY_VALUE_HEADS * HEAD_SIZE)
        .astype(jnp.bfloat16)
    )
    value_lowered = value_share.astype(jnp.bfloat16)
    first_back = (
        times_transposed(query_rounded, query_matrix)
        + times_transposed(key_lowered, key_projection)
        + times_transposed(value_lowered, value_projection)
    )
    first_gradient = jnp.sum(first_back * normed_one, axis=0)
    input_back = mixed_back + norm_back(
        first_back, normed_one, scale_one, first_scale.astype(jnp.float32)
    )
    full = (
        token_sum(hidden_first, query_rounded),
        token_sum(hidden_first, key_lowered),
        token_sum(hidden_first, value_lowered),
        token_sum(attention_result, mixed_low),
        token_sum(hidden_two, gate_back),
        token_sum(hidden_two, up_back),
        token_sum(activated, incoming_rows),
    )
    shares = (
        lax.psum_scatter(first_gradient, "wsh", scatter_dimension=0, tiled=True),
        lax.psum_scatter(full[0], "wsh", scatter_dimension=0, tiled=True),
        lax.psum_scatter(full[1], "wsh", scatter_dimension=0, tiled=True),
        lax.psum_scatter(full[2], "wsh", scatter_dimension=0, tiled=True),
        lax.psum_scatter(full[3], "wsh", scatter_dimension=0, tiled=True),
        lax.psum_scatter(second_gradient, "wsh", scatter_dimension=0, tiled=True),
        lax.psum_scatter(full[4], "wsh", scatter_dimension=0, tiled=True),
        lax.psum_scatter(full[5], "wsh", scatter_dimension=0, tiled=True),
        lax.psum_scatter(full[6], "wsh", scatter_dimension=0, tiled=True),
    )
    totals = lax.psum(
        (
            shares[0],
            shares[1],
            shares[2],
            shares[3],
            shares[4],
            shares[5],
            shares[6],
            shares[7],
            shares[8],
        ),
        "ctx",
    )
    return (
        layer_output[None],
        input_back[None],
        totals[0],
        totals[1],
        totals[2],
        totals[3],
        totals[4],
        totals[5],
        totals[6],
        totals[7],
        totals[8],
    )


def solution(mesh):
    in_specs = (
        P("wsh", "ctx", None),
        P(),
        P("wsh"),
        P("wsh", None),
        P("wsh", None),
        P("wsh", None),
        P("wsh", None),
        P("wsh"),
        P("wsh", None),
        P("wsh", None),
        P("wsh", None),
        P("wsh", "ctx", None),
    )
    out_specs = (
        P("wsh", "ctx", None),
        P("wsh", "ctx", None),
        P("wsh"),
        P("wsh", None),
        P("wsh", None),
        P("wsh", None),
        P("wsh", None),
        P("wsh"),
        P("wsh", None),
        P("wsh", None),
        P("wsh", None),
    )
    return jax.shard_map(
        per_device, mesh=mesh, in_specs=in_specs, out_specs=out_specs, check_vma=False
    )
```

profile of v0, /device:TPU:0, one launch (start us, length us, event | category | flops | bytes accessed | tf_op | source)
XLA Modules:
  0.0 1436.8 jit_solution(5317001073632541566)
XLA Ops:
  13.9 27.2 %all-gather.1 = bf16[4,240,320]{1,2,0:T(8,128)(2,1)S(1)} all-gather(bf16[1,240,320]{1,2,0:T(8,128)(2,1)S(1)} %bitcast.386), channel_id=1, replica_groups=mesh['ctx'=8,'wsh'=4] {'wsh'}, dimensions={0}, use_global_device_ids=true | all-gather | bytes 768000 | tf_op jit(solution)/shard_map/all_gather | solution.py:217
  44.0 12.7 all-reduce.7
  57.4 10.2 all_gather.38
  68.0 22.5 %all-gather = bf16[4,240,320]{1,2,0:T(8,128)(2,1)S(1)} all-gather(bf16[1,240,320]{1,2,0:T(8,128)(2,1)S(1)} %bitcast.387), channel_id=1, replica_groups=mesh['ctx'=8,'wsh'=4] {'wsh'}, dimensions={0}, use_global_device_ids=true | all-gather | bytes 768000 | tf_op jit(solution)/shard_map/all_gather | solution.py:216
  92.4 10.4 all_gather.35
  105.6 2.1 copy.83
  108.5 1.7 copy.87
  110.2 2.1 reshape_reshape.13
  112.5 3.8 copy.84
  116.3 2.3 fusion.96
  119.6 6.1 while.57
  126.0 1.5 while.56
  127.8 2.6 multiply_reduce_fusion.2
  130.8 77.1 %all-gather.12.cloned.1.call-done = bf16[960,2560]{1,0:T(8,128)(2,1)} async-done(((bf16[240,2560]{1,0:T(8,128)(2,1)}), bf16[960,2560]{1,0:T(8,128)(2,1)}) %all-gather.12.cloned.1.call-update) | async-done | bytes 4915216 | tf_op jit(solution)/shard_map/all_gather | solution.py:220
  207.9 4.3 fusion.125
  212.2 88.1 %all-gather.14.cloned.1.call-done = bf16[960,2560]{1,0:T(8,128)(2,1)} async-done(((bf16[240,2560]{1,0:T(8,128)(2,1)}), bf16[960,2560]{1,0:T(8,128)(2,1)}) %all-gather.14.cloned.1.call-update) | async-done | bytes 4915216 | tf_op jit(solution)/shard_map/all_gather | solution.py:221
  300.3 4.4 fusion.126
  304.8 88.0 %all-gather.16.cloned.1.call-done = bf16[2560,960]{0,1:T(8,128)(2,1)} async-done(((bf16[640,960]{0,1:T(8,128)(2,1)}), bf16[2560,960]{0,1:T(8,128)(2,1)}) %all-gather.16.cloned.1.call-update) | async-done | bytes 4915216 | tf_op jit(solution)/shard_map/all_gather | solution.py:222
  392.8 5.0 multiply_convert_fusion
  397.8 4.3 fusion.127
  402.2 1.5 multiply_reduce_fusion
  406.3 4.9 while.58
  411.2 19.3 %while.59 = (s32[]{:T(128)}, f32[64,5,3,64]{0,3,2,1:T(8,128)S(1)}, f32[1024,5,64]{0,2,1:T(8,128)S(1)}, f32[1024,5,64]{0,2,1:T(8,128)S(1)}, s32[]{:T(128)}, /*ind...) while((s32[]{:T(128)}, f32[64,5,3,64]{0,3,2,1:T(8,128)S(1)}, ...), condition=%wide.region_18.20_spmd, body=%wide.region_17.19_spmd.sunk | while | flops 159494144 | bytes 8113159 | solution.py:185
  411.4 1.4 fusion.254
  416.2 1.4 fusion.254
  421.0 1.4 fusion.254
  425.8 1.4 fusion.254
  430.6 2.2 reshape.379
  432.8 3.2 copy.90
  436.0 2.2 reshape.381
  438.2 3.4 copy.92
  441.6 2.2 gather_fusion.3
  443.8 4.1 gather_fusion.4
  447.9 4.9 broadcast_select_fusion.1
  452.8 2.3 copy.91
  455.1 1.7 reshape_reshape.14
  456.9 3.2 copy.93
  460.2 3.0 reshape_reshape.15
  463.3 29.3 %reduce-scatter.14.cloned.1.call-done = f32[128,320]{0,1:T(8,128)} async-done(((f32[1024,320]{0,1:T(8,128)}), f32[128,320]{0,1:T(8,128)}) %reduce-scatter.14.cloned.1.call-update) | async-done | bytes 163856 | tf_op jit(solution)/shard_map/reduce_scatter | solution.py:377
  493.6 1.5 fusion.100
  495.2 38.5 %reduce-scatter.16.cloned.1.call-done = f32[128,320]{0,1:T(8,128)} async-done(((f32[1024,320]{0,1:T(8,128)}), f32[128,320]{0,1:T(8,128)}) %reduce-scatter.16.cloned.1.call-update) | async-done | bytes 163856 | tf_op jit(solution)/shard_map/reduce_scatter | solution.py:385
  533.7 2.4 fusion.107
  536.5 2.7 fusion.102
  540.2 2.6 fusion.104
  544.1 5.2 fusion.129
  550.3 5.1 fusion.130
  556.6 5.2 fusion.92
  561.8 8.6 reduce-scatter.28.cloned.1.call-done
  570.5 1.9 copy.111
  572.3 33.8 %reduce-scatter.30.cloned.1.call-done = f32[240,320]{1,0:T(8,128)} async-done(((f32[960,320]{1,0:T(8,128)}), f32[240,320]{1,0:T(8,128)}) %reduce-scatter.30.cloned.1.call-update) | async-done | bytes 307216
  606.1 1.9 copy.113
  608.0 71.7 %reduce-scatter.18.cloned.1.call-done = f32[240,960]{1,0:T(8,128)} async-done(((f32[960,960]{1,0:T(8,128)}), f32[240,960]{1,0:T(8,128)}) %reduce-scatter.18.cloned.1.call-update) | async-done | bytes 921616 | tf_op jit(solution)/shard_map/reduce_scatter | solution.py:429
  679.7 75.4 %reduce-scatter.20.cloned.1.call-done = f32[240,960]{1,0:T(8,128)} async-done(((f32[960,960]{1,0:T(8,128)}), f32[240,960]{1,0:T(8,128)}) %reduce-scatter.20.cloned.1.call-update) | async-done | bytes 921616 | tf_op jit(solution)/shard_map/reduce_scatter | solution.py:432
  755.1 170.2 %reduce-scatter.22.cloned.1.call-done = f32[240,2560]{1,0:T(8,128)} async-done(((f32[960,2560]{1,0:T(8,128)}), f32[240,2560]{1,0:T(8,128)}) %reduce-scatter.22.cloned.1.call-update) | async-done | bytes 2457616 | tf_op jit(solution)/shard_map/reduce_scatter | solution.py:434
  925.3 170.9 %reduce-scatter.24.cloned.1.call-done = f32[240,2560]{1,0:T(8,128)} async-done(((f32[960,2560]{1,0:T(8,128)}), f32[240,2560]{1,0:T(8,128)}) %reduce-scatter.24.cloned.1.call-update) | async-done | bytes 2457616 | tf_op jit(solution)/shard_map/reduce_scatter | solution.py:435
  1096.1 170.7 %reduce-scatter.26.cloned.1.call-done = f32[640,960]{0,1:T(8,128)} async-done(((f32[2560,960]{0,1:T(8,128)}), f32[640,960]{0,1:T(8,128)}) %reduce-scatter.26.cloned.1.call-update) | async-done | bytes 2457616 | tf_op jit(solution)/shard_map/reduce_scatter | solution.py:436
  1267.9 4.6 fusion.74
  1274.9 11.7 all-reduce.6
  1286.7 13.2 all-reduce.4
  1300.9 117.6 %all-reduce.10.cloned.1.call-done = (f32[240,960]{1,0:T(8,128)}, f32[240,320]{0,1:T(8,128)}, f32[240,320]{0,1:T(8,128)}, f32[240,960]{1,0:T(8,128)}, f32[240,256...) async-done(((f32[240,960]{1,0:T(8,128)}, f32[240,320]{0,1:T(8,128)}, f32[240,320]{0,1:T(8,128)}, f32[240,960]{1,0:T(8,128)}, f32[240,2560]{1,0:T(8,128)}, ...) | async-done | bytes 9830416 | tf_op jit(solution)/shard_map/psum | solution.py:438
  1418.5 2.4 copy.175
  1423.3 1.4 copy.179
  1425.8 1.4 copy.180
  1428.4 1.4 copy.181
  (291 shorter events, 57.6 us)
Async XLA Ops:
  7.2 105.3 %all-gather.8.cloned.1.call-start = ((), (), s32[]{:S(2)}) async-start(), calls=%async_computation.9 | async-start | bytes 2457600 | tf_op jit(solution)/shard_map/all_gather | solution.py:215
  7.9 119.9 %all-gather.10.cloned.1.call-start = ((), (), s32[]{:S(2)}) async-start(), calls=%async_computation.10 | async-start | bytes 2457600 | tf_op jit(solution)/shard_map/all_gather | solution.py:218
  8.7 2.0 copy-start.46
  8.7 5.3 copy-start.44
  8.7 199.2 %all-gather.12.cloned.1.call-start = ((), (), s32[]{:S(2)}) async-start(), calls=%async_computation.11 | async-start | bytes 6144000 | tf_op jit(solution)/shard_map/all_gather | solution.py:220
  9.4 290.9 %all-gather.14.cloned.1.call-start = ((), (), s32[]{:S(2)}) async-start(), calls=%async_computation.12 | async-start | bytes 6144000 | tf_op jit(solution)/shard_map/all_gather | solution.py:221
  10.0 382.8 %all-gather.16.cloned.1.call-start = ((), (), s32[]{:S(2)}) async-start(), calls=%async_computation.13 | async-start | bytes 6144000 | tf_op jit(solution)/shard_map/all_gather | solution.py:222
  10.6 31.7 %copy-start.47 = (u32[32]{0:T(128)S(1)}, u32[32]{0:T(128)}, u32[]{:S(2)}) copy-start(u32[32]{0:T(128)} %constant.168) | copy-start | bytes 388
  10.6 32.9 %copy-start.48 = (bf16[240]{0:T(256)(128)(2,1)S(1)}, bf16[240]{0:T(256)(128)(2,1)}, u32[]{:S(2)}) copy-start(bf16[240]{0:T(256)(128)(2,1)} %param.26) | copy-start | bytes 1444
  10.6 33.2 %copy-start.49 = (bf16[240]{0:T(256)(128)(2,1)S(1)}, bf16[240]{0:T(256)(128)(2,1)}, u32[]{:S(2)}) copy-start(bf16[240]{0:T(256)(128)(2,1)} %param.31) | copy-start | bytes 1444
  10.6 46.1 %copy-start.5 = (bf16[1,128,960]{1,2,0:T(8,128)(2,1)S(1)}, bf16[1,128,960]{1,2,0:T(8,128)(2,1)}, u32[]{:S(2)}) copy-start(bf16[1,128,960]{1,2,0:T(8,128)(2,1)} %param.24) | copy-start | bytes 737284
  10.6 482.0 %reduce-scatter.14.cloned.1.call-start = ((), (), s32[]{:S(2)}) async-start(), calls=%async_computation.14 | async-start | bytes 1474560 | tf_op jit(solution)/shard_map/reduce_scatter | solution.py:377
  42.2 48.3 %copy-start.30 = (bf16[960,320]{0,1:T(8,128)(2,1)}, bf16[960,320]{0,1:T(8,128)(2,1)S(1)}, u32[]{:S(2)}) copy-start(bf16[960,320]{0,1:T(8,128)(2,1)S(1)} %reshape.437) | copy-start | bytes 1843204
  42.2 25.7 %copy-start.45 = (bf16[240,320]{0,1:T(8,128)(2,1)S(1)}, bf16[240,320]{0,1:T(8,128)(2,1)}, u32[]{:S(2)}) copy-start(bf16[240,320]{0,1:T(8,128)(2,1)} %param.28) | copy-start | bytes 460804
  91.6 11.9 copy-start.22
  105.6 2.9 copy-start.24
  118.9 6.9 copy-start.14
  127.5 3.0 copy-start.3
  127.5 3.0 copy-start.4
  127.8 84.4 %copy-start.35 = (bf16[128,5,3,64]{0,3,2,1:T(8,128)(2,1)}, bf16[128,5,3,64]{0,3,2,1:T(8,128)(2,1)S(1)}, u32[]{:S(2)}) copy-start(bf16[128,5,3,64]{0,3,2,1:T(8,128)(2,1)S(1)} %pad_maximum_fusion.2) | copy-start | bytes 737284
  130.5 273.3 %copy-start.10 = (f32[128,960]{0,1:T(8,128)}, f32[128,960]{0,1:T(8,128)S(1)}, u32[]{:S(2)}) copy-start(f32[128,960]{0,1:T(8,128)S(1)} %get-tuple-element.528) | copy-start | bytes 1474564
  130.8 169.6 %copy-start.20 = (bf16[128,960]{0,1:T(8,128)(2,1)}, bf16[128,960]{0,1:T(8,128)(2,1)S(1)}, u32[]{:S(2)}) copy-start(bf16[128,960]{0,1:T(8,128)(2,1)S(1)} %multiply_convert_fusion.3) | copy-start | bytes 737284
  212.2 180.6 %copy-start.38 = (bf16[1,128,960]{1,2,0:T(8,128)(2,1)S(1)}, bf16[1,128,960]{1,2,0:T(8,128)(2,1)}, u32[]{:S(2)}) copy-start(bf16[1,128,960]{1,2,0:T(8,128)(2,1)} %param.35) | copy-start | bytes 737284
  300.3 92.5 %copy-start.37 = (f32[128,2560]{1,0:T(8,128)S(1)}, f32[128,2560]{1,0:T(8,128)}, u32[]{:S(2)}) copy-start(f32[128,2560]{1,0:T(8,128)} %fusion.125) | copy-start | bytes 3932164
  397.8 4.4 copy-start.28
  397.8 4.4 copy-start.26
  397.8 4.4 copy-start.7
  402.2 1.8 copy-start.17
  404.0 1.1 copy-start.18
  404.8 1.5 copy-start.15
  406.3 2.8 copy-start
  412.9 2.6 copy-start.13
  417.6 2.6 copy-start.13
  422.4 2.6 copy-start.13
  427.2 2.6 copy-start.13
  438.2 3.4 copy-start.8
  443.8 4.1 copy-start.9
  456.9 76.8 %reduce-scatter.16.cloned.1.call-start = ((), (), s32[]{:S(2)}) async-start(), calls=%async_computation.15 | async-start | bytes 1474560 | tf_op jit(solution)/shard_map/reduce_scatter | solution.py:385
  460.2 33.4 %copy-start.6 = (bf16[1,128,960]{1,2,0:T(8,128)(2,1)S(1)}, bf16[1,128,960]{1,2,0:T(8,128)(2,1)}, u32[]{:S(2)}) copy-start(bf16[1,128,960]{1,2,0:T(8,128)(2,1)} %param.24) | copy-start | bytes 737284
  463.2 107.2 %reduce-scatter.28.cloned.1.call-start = ((), (), s32[]{:S(2)}) async-start(), calls=%async_computation.21 | async-start | bytes 1843200
  495.1 41.0 %copy-start.2 = (f32[64,5,3,64]{0,3,2,1:T(8,128)S(1)}, f32[64,5,3,64]{0,3,2,1:T(8,128)}, u32[]{:S(2)}) copy-start(f32[64,5,3,64]{0,3,2,1:T(8,128)} %get-tuple-element.268) | copy-start | bytes 737284
  495.1 111.0 %reduce-scatter.30.cloned.1.call-start = ((), (), s32[]{:S(2)}) async-start(), calls=%async_computation.22 | async-start | bytes 1843200
  536.1 143.6 %reduce-scatter.18.cloned.1.call-start = ((), (), s32[]{:S(2)}) async-start(), calls=%async_computation.16 | async-start | bytes 4915200 | tf_op jit(solution)/shard_map/reduce_scatter | solution.py:429
  539.2 1.1 copy-start.36
  539.2 215.9 %reduce-scatter.20.cloned.1.call-start = ((), (), s32[]{:S(2)}) async-start(), calls=%async_computation.17 | async-start | bytes 4915200 | tf_op jit(solution)/shard_map/reduce_scatter | solution.py:432
  542.8 1.2 copy-start.29
  542.8 382.4 %reduce-scatter.22.cloned.1.call-start = ((), (), s32[]{:S(2)}) async-start(), calls=%async_computation.18 | async-start | bytes 12288000 | tf_op jit(solution)/shard_map/reduce_scatter | solution.py:434
  549.2 1.1 copy-start.27
  549.3 546.9 %reduce-scatter.24.cloned.1.call-start = ((), (), s32[]{:S(2)}) async-start(), calls=%async_computation.19 | async-start | bytes 12288000 | tf_op jit(solution)/shard_map/reduce_scatter | solution.py:435
  555.5 1.1 copy-start.25
  555.5 1.1 copy-start.39
  555.5 711.4 %reduce-scatter.26.cloned.1.call-start = ((), (), s32[]{:S(2)}) async-start(), calls=%async_computation.20 | async-start | bytes 12288000 | tf_op jit(solution)/shard_map/reduce_scatter | solution.py:436
  561.8 856.7 %all-reduce.10.cloned.1.call-start = ((), (), s32[]{:S(2)}) async-start(), calls=%async_computation.23 | async-start | bytes 19988480 | tf_op jit(solution)/shard_map/psum | solution.py:438
  1266.9 1.0 copy-start.11
  1267.9 4.7 copy-start.23
  1267.9 5.1 copy-start.31
  1267.9 5.1 copy-start.41
  1272.6 1.5 copy-start.16
  1418.5 2.4 copy-start.43
  1418.5 3.1 copy-start.42
  1418.5 3.8 copy-start.40
  1420.9 2.4 copy-start.34
  1423.3 2.6 copy-start.33
  1425.8 2.6 copy-start.32
  (4 other events, 3.5 us)
Sparse Core Ops, SparseCore 0:
  9.6 53.6 all-gather.7
  64.8 50.6 all-gather.9
  117.1 90.7 all-gather.11
  209.3 91.0 all-gather.13
  301.8 91.0 all-gather.15
  457.0 35.5 reduce-scatter.13
  496.4 37.1 reduce-scatter.15
  536.5 33.8 reduce-scatter.27
  573.4 32.7 reduce-scatter.29
  608.3 71.3 reduce-scatter.17
  682.0 73.0 reduce-scatter.19
  757.3 167.8 reduce-scatter.21
  927.6 168.4 reduce-scatter.23
  1098.4 168.4 reduce-scatter.25
  1272.3 146.1 all-reduce.9
where the time goes:
time: 1450 us; the launch traced here: 1440 us
  waiting for transfers between devices  1140 us (79%)
  blocking collectives  108 us (7%)
  matrix products  83.9 us (6%)
  local copies, waits for them, and re-layouts  67.9 us (5%)
  between operations  17.9 us (1%)
    reduce_scatter x1, waiting for transfers between devices, per_device(): lax.psum_scatter(full[5], 'wsh', scatter_dimension=0, tiled=True)  171 us
    reduce_scatter x1, waiting for transfers between devices, per_device(): lax.psum_scatter(full[6], 'wsh', scatter_dimension=0, tiled=True)  171 us
    reduce_scatter x1, waiting for transfers between devices, per_device(): lax.psum_scatter(full[4], 'wsh', scatter_dimension=0, tiled=True)  170 us
    psum x1, waiting for transfers between devices, per_device(): lax.psum((shares[0], shares[1], shares[2], shares[3], shares[4], shares[5...  118 us
    all_gather x1, waiting for transfers between devices, per_device(): lax.all_gather(shards[7], 'wsh', axis=0, tiled=True)  88.1 us
    all_gather x1, waiting for transfers between devices, per_device(): lax.all_gather(shards[8], 'wsh', axis=0, tiled=True)  88 us
    all_gather x1, waiting for transfers between devices, per_device(): lax.all_gather(shards[6], 'wsh', axis=0, tiled=True)  77.1 us
    reduce_scatter x1, waiting for transfers between devices, per_device(): lax.psum_scatter(full[3], 'wsh', scatter_dimension=0, tiled=True)  75.4 us
  transfers between devices with their start and end apart: 15, of which 13 were waited for; matrix products, arithmetic and copies ran while one was open for 6% of the time, Pallas kernels for 0%

commit v1 on v0

--- a/solution.py
+++ b/solution.py
@@ -13,6 +13,16 @@
 EPS = 1e-05
 ROPE_BASE = 10000.0
 NEG_FILL = -1e30
+KV_SEND = jnp.bfloat16
+
+
+def gather_all(piece):
+    return lax.all_gather(piece, ("wsh", "ctx"), axis=0, tiled=False)
+
+
+def scatter_all(pieces):
+    near = lax.psum_scatter(pieces, "ctx", scatter_dimension=0, tiled=False)
+    return lax.psum_scatter(near, "wsh", scatter_dimension=0, tiled=False)
 
 
 def matrix_product(left, right):
@@ -199,39 +209,35 @@
     down_weight,
     cotangent,
 ):
-    shards = (
-        first_gain,
-        query_weight,
-        key_weight,
-        value_proj_weight,
-        output_weight,
-        second_gain,
-        gate_weight,
-        up_weight,
-        down_weight,
-    )
-    gathered = (
-        lax.all_gather(shards[0], "wsh", axis=0, tiled=True),
-        lax.all_gather(shards[1], "wsh", axis=0, tiled=True),
-        lax.all_gather(shards[2], "wsh", axis=0, tiled=True),
-        lax.all_gather(shards[3], "wsh", axis=0, tiled=True),
-        lax.all_gather(shards[4], "wsh", axis=0, tiled=True),
-        lax.all_gather(shards[5], "wsh", axis=0, tiled=True),
-        lax.all_gather(shards[6], "wsh", axis=0, tiled=True),
-        lax.all_gather(shards[7], "wsh", axis=0, tiled=True),
-        lax.all_gather(shards[8], "wsh", axis=0, tiled=True),
-    )
-    (
-        first_scale,
-        query_matrix,
-        key_projection,
-        value_projection,
-        output_matrix,
-        second_scale,
-        gate_matrix,
-        up_matrix,
-        down_matrix,
-    ) = gathered
+    parts = lax.axis_size("ctx")
+    groups = lax.axis_size("wsh")
+    spot = lax.axis_index("ctx")
+
+    def spread(shard, columns):
+        rows, width = shard.shape
+        if columns:
+            piece = lax.dynamic_slice_in_dim(shard, spot * (width // parts), width // parts, 1)
+        else:
+            piece = lax.dynamic_slice_in_dim(shard, spot * (rows // parts), rows // parts, 0)
+        pieces = gather_all(piece)
+        if columns:
+            return (
+                pieces.reshape(groups, parts, rows, width // parts)
+                .transpose(0, 2, 1, 3)
+                .reshape(groups * rows, width)
+            )
+        return pieces.reshape(groups * rows, width)
+
+    gains = lax.all_gather(jnp.stack([first_gain, second_gain]), "wsh", axis=0, tiled=False)
+    gains = gains.transpose(1, 0, 2).reshape(2, -1)
+    first_scale, second_scale = gains[0], gains[1]
+    first_matrices = spread(jnp.concatenate([query_weight, key_weight, value_proj_weight], axis=1), True)
+    query_width = query_weight.shape[1]
+    key_width = key_weight.shape[1]
+    output_matrix = spread(output_weight, True)
+    wide_matrices = spread(jnp.concatenate([gate_weight, up_weight], axis=1), True)
+    down_matrix = spread(down_weight, False)
+    hidden_units = gate_weight.shape[1]
     tokens = layer_input[0]
     incoming_rows = cotangent[0]
     worker_rows = tokens.shape[0]
@@ -248,27 +254,27 @@
     scale_one = norm_scale(inputs)
     normed_one = inputs * scale_one
     hidden_first = (normed_one * first_scale.astype(jnp.float32)).astype(jnp.bfloat16)
+    projected = matrix_product(hidden_first, first_matrices)
     query_rows_local = apply_rotary(
-        matrix_product(hidden_first, query_matrix).reshape(worker_rows, QUERY_HEADS, HEAD_SIZE),
+        projected[:, :query_width].reshape(worker_rows, QUERY_HEADS, HEAD_SIZE),
         cosine_table,
         sine_table,
     ).astype(jnp.bfloat16)
     keys_rotated_pos = apply_rotary(
-        matrix_product(hidden_first, key_projection).reshape(
+        projected[:, query_width : query_width + key_width].reshape(
             worker_rows, KEY_VALUE_HEADS, HEAD_SIZE
         ),
         cosine_table,
         sine_table,
     ).astype(jnp.bfloat16)
-    value_rows_local = matrix_product(hidden_first, value_projection).astype(jnp.bfloat16)
-    keys_gathered_full, values_gathered_full = (
-        lax.all_gather(
-            keys_rotated_pos.reshape(worker_rows, KEY_VALUE_HEADS * HEAD_SIZE),
-            "ctx",
-            axis=0,
-            tiled=True,
+    value_rows_local = projected[:, query_width + key_width :].astype(jnp.bfloat16)
+    both = lax.all_gather(
+        jnp.concatenate(
+            [keys_rotated_pos.reshape(worker_rows, key_width), value_rows_local], axis=1
         ),
-        lax.all_gather(value_rows_local, "ctx", axis=0, tiled=True),
+        "ctx",
+        axis=0,
+        tiled=True,
     )
     block_count = sequence_rows // half_rows
     block_ids = positions.reshape(block_count, half_rows)[:, 0] // half_rows
@@ -285,10 +291,9 @@
             array.reshape((block_count, half_rows) + array.shape[1:]), block_ids, axis=0
         ).reshape(array.shape)
 
-    keys_ordered = ordered_blocks(keys_gathered_full).reshape(
-        sequence_rows, KEY_VALUE_HEADS, HEAD_SIZE
-    )
-    values_ordered = ordered_blocks(values_gathered_full).reshape(
+    both_ordered = ordered_blocks(both)
+    keys_ordered = both_ordered[:, :key_width].reshape(sequence_rows, KEY_VALUE_HEADS, HEAD_SIZE)
+    values_ordered = both_ordered[:, key_width:].reshape(
         sequence_rows, KEY_VALUE_HEADS, HEAD_SIZE
     )
     places_sorted = ordered_blocks(positions)
@@ -322,8 +327,9 @@
     scale_two = norm_scale(mixed)
     normed_two = mixed * scale_two
     hidden_two = (normed_two * second_scale.astype(jnp.float32)).astype(jnp.bfloat16)
-    gate = matrix_product(hidden_two, gate_matrix)
-    upward = matrix_product(hidden_two, up_matrix)
+    wide = matrix_product(hidden_two, wide_matrices)
+    gate = wide[:, :hidden_units]
+    upward = wide[:, hidden_units:]
     sigma = jax.nn.sigmoid(gate)
     activated = (gate * sigma * upward).astype(jnp.bfloat16)
     layer_output = (mixed + matrix_product(activated, down_matrix)).astype(jnp.bfloat16)
@@ -332,7 +338,8 @@
         jnp.bfloat16
     )
     up_back = (activated_back * gate * sigma).astype(jnp.bfloat16)
-    second_back = times_transposed(gate_back, gate_matrix) + times_transposed(up_back, up_matrix)
+    wide_back = jnp.concatenate([gate_back, up_back], axis=1)
+    second_back = times_transposed(wide_back, wide_matrices)
     second_gradient = jnp.sum(second_back * normed_two, axis=0)
     mixed_back = incoming_rows.astype(jnp.float32) + norm_back(
         second_back, normed_two, scale_two, second_scale.astype(jnp.float32)
@@ -373,24 +380,22 @@
     query_gradient_back = jnp.concatenate(query_parts, axis=0).reshape(
         worker_rows, QUERY_HEADS, HEAD_SIZE
     )
-    key_portion_local, value_share = (
-        lax.psum_scatter(
-            blocks_per_worker(keys_gradient_back).reshape(
-                sequence_rows, KEY_VALUE_HEADS * HEAD_SIZE
-            ),
-            "ctx",
-            scatter_dimension=0,
-            tiled=True,
+    both_share = lax.psum_scatter(
+        blocks_per_worker(
+            jnp.concatenate(
+                [
+                    keys_gradient_back.reshape(sequence_rows, key_width),
+                    values_gradient_back.reshape(sequence_rows, key_width),
+                ],
+                axis=1,
+            ).astype(KV_SEND)
         ),
-        lax.psum_scatter(
-            blocks_per_worker(values_gradient_back).reshape(
-                sequence_rows, KEY_VALUE_HEADS * HEAD_SIZE
-            ),
-            "ctx",
-            scatter_dimension=0,
-            tiled=True,
-        ),
-    )
+        "ctx",
+        scatter_dimension=0,
+        tiled=True,
+    ).astype(jnp.float32)
+    key_portion_local = both_share[:, :key_width]
+    value_share = both_share[:, key_width:]
     query_rounded = (
         apply_rotary_back(query_gradient_back, cosine_table, sine_table)
         .reshape(worker_rows, QUERY_HEADS * HEAD_SIZE)
@@ -406,61 +411,45 @@
         .astype(jnp.bfloat16)
     )
     value_lowered = value_share.astype(jnp.bfloat16)
-    first_back = (
-        times_transposed(query_rounded, query_matrix)
-        + times_transposed(key_lowered, key_projection)
-        + times_transposed(value_lowered, value_projection)
-    )
+    first_cols = jnp.concatenate([query_rounded, key_lowered, value_lowered], axis=1)
+    first_back = times_transposed(first_cols, first_matrices)
     first_gradient = jnp.sum(first_back * normed_one, axis=0)
     input_back = mixed_back + norm_back(
         first_back, normed_one, scale_one, first_scale.astype(jnp.float32)
     )
-    full = (
-        token_sum(hidden_first, query_rounded),
-        token_sum(hidden_first, key_lowered),
-        token_sum(hidden_first, value_lowered),
-        token_sum(attention_result, mixed_low),
-        token_sum(hidden_two, gate_back),
-        token_sum(hidden_two, up_back),
-        token_sum(activated, incoming_rows),
-    )
-    shares = (
-        lax.psum_scatter(first_gradient, "wsh", scatter_dimension=0, tiled=True),
-        lax.psum_scatter(full[0], "wsh", scatter_dimension=0, tiled=True),
-        lax.psum_scatter(full[1], "wsh", scatter_dimension=0, tiled=True),
-        lax.psum_scatter(full[2], "wsh", scatter_dimension=0, tiled=True),
-        lax.psum_scatter(full[3], "wsh", scatter_dimension=0, tiled=True),
-        lax.psum_scatter(second_gradient, "wsh", scatter_dimension=0, tiled=True),
-        lax.psum_scatter(full[4], "wsh", scatter_dimension=0, tiled=True),
-        lax.psum_scatter(full[5], "wsh", scatter_dimension=0, tiled=True),
-        lax.psum_scatter(full[6], "wsh", scatter_dimension=0, tiled=True),
-    )
-    totals = lax.psum(
-        (
-            shares[0],
-            shares[1],
-            shares[2],
-            shares[3],
-            shares[4],
-            shares[5],
-            shares[6],
-            shares[7],
-            shares[8],
-        ),
-        "ctx",
-    )
+
+    def collect(gradient, columns):
+        rows, width = gradient.shape
+        own_rows = rows // groups
+        sent = gradient.astype(jnp.bfloat16)
+        if columns:
+            sent = sent.reshape(groups, own_rows, parts, width // parts).transpose(2, 0, 1, 3)
+        else:
+            sent = sent.reshape(groups, parts, own_rows // parts, width).transpose(1, 0, 2, 3)
+        pieces = lax.all_gather(scatter_all(sent), "ctx", axis=0, tiled=False)
+        if columns:
+            pieces = pieces.transpose(1, 0, 2)
+        return pieces.reshape(own_rows, width).astype(jnp.float32)
+
+    down_total = collect(token_sum(activated, incoming_rows), False)
+    wide_total = collect(token_sum(hidden_two, wide_back), True)
+    output_total = collect(token_sum(attention_result, mixed_low), True)
+    first_total = collect(token_sum(hidden_first, first_cols), True)
+    gain_sums = lax.psum(jnp.stack([first_gradient, second_gradient]), ("wsh", "ctx"))
+    own_gain = first_gain.shape[0]
+    gain_sums = lax.dynamic_slice_in_dim(gain_sums, lax.axis_index("wsh") * own_gain, own_gain, 1)
     return (
         layer_output[None],
         input_back[None],
-        totals[0],
-        totals[1],
-        totals[2],
-        totals[3],
-        totals[4],
-        totals[5],
-        totals[6],
-        totals[7],
-        totals[8],
+        gain_sums[0],
+        first_total[:, :query_width],
+        first_total[:, query_width : query_width + key_width],
+        first_total[:, query_width + key_width :],
+        output_total,
+        gain_sums[1],
+        wide_total[:, :hidden_units],
+        wide_total[:, hidden_units:],
+        down_total,
     )
 
 

time: 1450 us -> 840 us (0.58)
  waiting for transfers between devices: 1140 us -> 479 us
  local copies, waits for them, and re-layouts: 67.9 us -> 149 us
  blocking collectives: 108 us -> 73.1 us
  other arithmetic: 13.9 us -> 30.6 us
    reduce_scatter x7, waiting for transfers between devices: 727 us -> 211 us  [the longest x3 150 us: scatter_all(): near = lax.psum_scatter(pieces, 'ctx', scatter_dimension=0, tiled=False)]
    psum x1 -> x0, waiting for transfers between devices: 118 us -> none  [per_device(): lax.psum((shares[0], shares[1], shares[2], shares[3], shares[4], shares[5...]
    reshape x4 -> x9, local copies, waits for them, and re-layouts: 11 us -> 54.9 us  [the longest x5 33.2 us: collect(): sent.reshape(groups, own_rows, parts, width // parts).transpose(2, 0, 1, 3)]
    all_gather x5 -> x7, waiting for transfers between devices: 253 us -> 216 us  [the longest x4 180 us: gather_all(): return lax.all_gather(piece, ('wsh', 'ctx'), axis=0, tiled=False)]
    all_gather x4 -> x3, blocking collectives: 70.4 us -> 34.1 us  [the longest x2 21.5 us: collect(): pieces = lax.all_gather(scatter_all(sent), 'ctx', axis=0, tiled=False)]
    psum x1, blocking collectives: 13.2 us -> 39 us  [per_device(): lax.psum(jnp.stack([first_gradient, second_gradient]), ('wsh', 'ctx'))]
    unnamed x2 -> x0, blocking collectives: 24.4 us -> none
    unnamed x112 -> x117, local copies, waits for them, and re-layouts: 23.1 us -> 35.7 us
  transfers between devices with their start and end apart: 15 -> 16, of which waited for: 13 -> 14; matrix products, arithmetic and copies ran while one was open for 6% -> 24% of each run, Pallas kernels for 0% -> 0%
where the time goes in v1:
time: 840 us; the launch traced here: 828 us
  waiting for transfers between devices  479 us (57%)
  local copies, waits for them, and re-layouts  149 us (18%)
  matrix products  77.9 us (9%)
  blocking collectives  73.1 us (9%)
  other arithmetic  30.6 us (4%)
  between operations  16.7 us (2%)
    all_gather x4, waiting for transfers between devices, gather_all(): return lax.all_gather(piece, ('wsh', 'ctx'), axis=0, tiled=False)  180 us
    reduce_scatter x3, waiting for transfers between devices, scatter_all(): near = lax.psum_scatter(pieces, 'ctx', scatter_dimension=0, tiled=False)  150 us
    reduce_scatter x4, waiting for transfers between devices, scatter_all(): return lax.psum_scatter(near, 'wsh', scatter_dimension=0, tiled=False)  60.8 us
    unnamed x18, waiting for transfers between devices  51.7 us
    psum x1, blocking collectives, per_device(): lax.psum(jnp.stack([first_gradient, second_gradient]), ('wsh', 'ctx'))  39 us
    unnamed x117, local copies, waits for them, and re-layouts  35.7 us
    reshape x5, local copies, waits for them, and re-layouts, collect(): sent.reshape(groups, own_rows, parts, width // parts).transpose(2, 0, 1, 3)  33.2 us
    all_gather x2, blocking collectives, collect(): pieces = lax.all_gather(scatter_all(sent), 'ctx', axis=0, tiled=False)  21.5 us
  transfers between devices with their start and end apart: 16, of which 14 were waited for; matrix products, arithmetic and copies ran while one was open for 24% of the time, Pallas kernels for 0%

profile of v1, /device:TPU:0, one launch (start us, length us, event | category | flops | bytes accessed | tf_op | source)
XLA Modules:
  0.0 828.4 jit_solution(15796384509911260445)
XLA Ops:
  13.5 12.7 %all-gather.5 = bf16[4,2,240]{2,1,0:T(2,128)(2,1)S(1)} all-gather(bf16[1,2,240]{2,1,0:T(2,128)(2,1)S(1)} %maximum_bitcast_fusion), channel_id=2, replica_groups=mesh['ctx'=8,'wsh'=4] {'wsh'}, dimensions={0}, use_global_device_ids=true | all-gather | bytes 4800 | tf_op jit(solution)/shard_map/all_gather | solution.py:231
  26.7 47.4 %all-gather.27.cloned.1.call-done = bf16[32,240,200]{1,2,0:T(8,128)(2,1)} async-done(((bf16[1,240,200]{1,2,0:T(8,128)(2,1)}), bf16[32,240,200]{1,2,0:T(8,128)(2,1)}) %all-gather.27.cloned.1.call-update) | async-done | bytes 3072016 | tf_op jit(solution)/shard_map/all_gather | solution.py:20
  74.1 6.2 copy.197
  80.2 7.4 reshape.397
  87.6 3.1 fusion.94
  99.8 32.5 %all-gather.21.cloned.1.call-done = bf16[7680,120]{1,0:T(8,128)(2,1)} async-done(((bf16[240,120]{1,0:T(8,128)(2,1)}), bf16[7680,120]{1,0:T(8,128)(2,1)}) %all-gather.21.cloned.1.call-update) | async-done | bytes 1843216 | tf_op jit(solution)/shard_map/all_gather | solution.py:20
  132.3 2.1 copy.253
  134.3 2.8 reshape.406
  138.8 19.4 %all-gather.15.cloned.1.call-done = bf16[1024,640]{0,1:T(8,128)(2,1)} async-done(((bf16[128,640]{0,1:T(8,128)(2,1)}), bf16[1024,640]{0,1:T(8,128)(2,1)}) %all-gather.15.cloned.1.call-update) | async-done | bytes 1310736 | tf_op jit(solution)/shard_map/all_gather | solution.py:271
  158.2 1.7 copy.198
  159.9 1.8 gather_fusion.1
  164.2 8.4 %while.57 = (s32[]{:T(128)}, f32[64,5,3]{0,2,1:T(4,128)S(1)}, f32[64,5,3]{0,2,1:T(4,128)S(1)}, f32[64,5,3,64]{0,3,2,1:T(8,128)S(1)}, s32[]{:T(128)}, /*index=5*/...) while((s32[]{:T(128)}, f32[64,5,3]{0,2,1:T(4,128)S(1)}, ...), condition=%wide.region_11.13_spmd, body=%wide.region_8.12_spmd.sunk | while | flops 64776068 | bytes 4370375 | solution.py:123
  173.9 6.3 while.56
  184.6 60.1 %all-gather.23.cloned.1.call-done = bf16[7680,640]{1,0:T(8,128)(2,1)} async-done(((bf16[240,640]{1,0:T(8,128)(2,1)}), bf16[7680,640]{1,0:T(8,128)(2,1)}) %all-gather.23.cloned.1.call-update) | async-done | bytes 9830416 | tf_op jit(solution)/shard_map/all_gather | solution.py:20
  244.7 9.5 %copy.204 = bf16[4,8,240,640]{3,1,2,0:T(8,128)(2,1)} copy(bf16[4,8,240,640]{3,2,1,0:T(8,128)(2,1)} %bitcast.398) | data formatting | bytes 19660800 | tf_op jit(solution)/shard_map/reshape | solution.py:225
  254.2 10.1 %copy.246 = bf16[120,8,8,640]{3,1,2,0:T(8,128)(2,1)} copy(bf16[120,8,8,640]{3,2,1,0:T(8,128)(2,1)} %bitcast.385) | data formatting | bytes 19660800
  264.3 7.0 fusion.113
  271.3 40.5 %all-gather.25.cloned.1.call-done = bf16[2560,960]{1,0:T(8,128)(2,1)} async-done(((bf16[80,960]{1,0:T(8,128)(2,1)}), bf16[2560,960]{1,0:T(8,128)(2,1)}) %all-gather.25.cloned.1.call-update) | async-done | bytes 4915216 | tf_op jit(solution)/shard_map/all_gather | solution.py:20
  311.9 6.4 multiply_convert_fusion.1
  318.3 3.4 multiply_reduce_fusion
  325.6 13.9 %while.58 = (s32[]{:T(128)}, f32[64,5,3,64]{0,3,2,1:T(8,128)S(1)}, f32[1024,5,64]{0,2,1:T(8,128)S(1)}, f32[1024,5,64]{0,2,1:T(8,128)}, s32[]{:T(128)}, /*index=5...) while((s32[]{:T(128)}, f32[64,5,3,64]{0,3,2,1:T(8,128)S(1)}, ...), condition=%wide.region_16.18_spmd, body=%wide.region_15.17_spmd.sunk | while | flops 159494144 | bytes 7397639 | solution.py:195
  330.6 2.0 fusion.219
  337.6 2.0 fusion.219
  339.5 5.0 convolution_convert_fusion.1
  344.6 7.9 copy.216
  353.4 22.9 %while.59 = (s32[]{:T(128)}, f32[64,5,3,64]{0,3,2,1:T(8,128)S(1)}, f32[1024,5,64]{0,2,1:T(8,128)S(1)}, f32[1024,5,64]{0,2,1:T(8,128)}, s32[]{:T(128)}, /*index=5...) while((s32[]{:T(128)}, f32[64,5,3,64]{0,3,2,1:T(8,128)S(1)}, ...), condition=%wide.region_18.20_spmd, body=%wide.region_17.19_spmd.sunk | while | flops 159494144 | bytes 7375851 | solution.py:195
  359.1 2.0 fusion.234
  366.7 2.0 fusion.234
  374.3 2.0 fusion.234
  377.7 1.9 concatenate.56
  379.5 1.9 copy.208
  382.4 1.9 concatenate.55
  384.3 1.7 copy.207
  386.0 1.7 pad_maximum_fusion.1
  387.7 1.9 gather_fusion.2
  389.6 2.6 broadcast_select_fusion
  393.5 5.4 convolution_convert_fusion
  398.9 9.9 %copy.247 = bf16[120,8,8,640]{3,2,1,0:T(8,128)(2,1)} copy(bf16[120,8,8,640]{3,1,2,0:T(8,128)(2,1)} %bitcast.383) | data formatting | bytes 19660800
  408.8 8.9 %copy.251 = bf16[4,240,8,640]{3,1,0,2:T(8,128)(2,1)} copy(bf16[4,240,8,640]{3,2,1,0:T(8,128)(2,1)} %bitcast.386) | data formatting | bytes 19660800 | tf_op jit(solution)/shard_map/reshape | solution.py:426
  418.8 1.9 convolution_convert_fusion.3
  420.8 5.0 reshape.415
  425.8 3.1 copy.252
  430.4 13.1 %all-reduce.3.cloned.1.call-done = bf16[8,4,80,960]{3,2,0,1:T(8,128)(2,1)} async-done(((bf16[8,4,80,960]{3,2,0,1:T(8,128)(2,1)}), bf16[8,4,80,960]{3,2,0,1:T(8,128)(2,1)}) %all-reduce.3.cloned.1.call-update) | async-done | bytes 4915216
  443.5 2.6 dynamic-slice_bitcast_fusion
  446.3 38.3 %reduce-scatter.26.cloned.1.call-done = bf16[128,640]{1,0:T(8,128)(2,1)} async-done(((bf16[1024,640]{1,0:T(8,128)(2,1)}), bf16[128,640]{1,0:T(8,128)(2,1)}) %reduce-scatter.26.cloned.1.call-update) | async-done | bytes 163856
  486.0 2.7 convolution_convert_fusion.2
  488.7 9.3 %reshape.485 = bf16[4,240,8,200]{3,2,1,0:T(8,128)(2,1)} reshape(bf16[960,1600]{1,0:T(8,128)(2,1)} %convolution_convert_fusion.2) | data formatting | bytes 6144000 | tf_op jit(solution)/shard_map/reshape | solution.py:426
  498.1 6.8 copy.237
  504.9 4.3 copy.211
  509.3 57.6 %reduce-scatter.20.cloned.1.call-done = bf16[1,4,240,640]{3,2,1,0:T(8,128)(2,1)} async-done(((bf16[8,4,240,640]{3,2,1,0:T(8,128)(2,1)}), bf16[1,4,240,640]{3,2,1,0:T(8,128)(2,1)}) %reduce-scatter.20.cloned.1.call-update) | async-done | bytes 1228816 | tf_op jit(solution)/shard_map/reduce_scatter | solution.py:24
  566.9 44.1 %reduce-scatter.16.cloned.1.call-done = bf16[1,4,240,120]{3,2,1,0:T(8,128)(2,1)} async-done(((bf16[8,4,240,120]{3,2,1,0:T(8,128)(2,1)}), bf16[1,4,240,120]{3,2,1,0:T(8,128)(2,1)}) %reduce-scatter.16.cloned.1.call-update) | async-done | bytes 230416 | tf_op jit(solution)/shard_map/reduce_scatter | solution.py:24
  611.1 25.3 %reduce-scatter.24.cloned.1.call-done = bf16[1,80,960]{2,1,0:T(8,128)(2,1)} async-done(((bf16[4,80,960]{2,1,0:T(8,128)(2,1)}), bf16[1,80,960]{2,1,0:T(8,128)(2,1)}) %reduce-scatter.24.cloned.1.call-update) | async-done | bytes 153616 | tf_op jit(solution)/shard_map/reduce_scatter | solution.py:25
  636.4 48.8 %reduce-scatter.12.cloned.1.call-done = bf16[1,4,240,200]{2,3,1,0:T(8,128)(2,1)} async-done(((bf16[8,4,240,200]{2,3,1,0:T(8,128)(2,1)}), bf16[1,4,240,200]{2,3,1,0:T(8,128)(2,1)}) %reduce-scatter.12.cloned.1.call-update) | async-done | bytes 384016 | tf_op jit(solution)/shard_map/reduce_scatter | solution.py:24
  685.5 32.1 %reduce-scatter.22.cloned.1.call-done = bf16[1,240,640]{2,1,0:T(8,128)(2,1)} async-done(((bf16[4,240,640]{2,1,0:T(8,128)(2,1)}), bf16[1,240,640]{2,1,0:T(8,128)(2,1)}) %reduce-scatter.22.cloned.1.call-update) | async-done | bytes 307216 | tf_op jit(solution)/shard_map/reduce_scatter | solution.py:25
  717.7 5.0 fusion.73
  724.2 39.0 %psum.7 = f32[2,960]{1,0:T(2,128)S(1)} all-reduce(f32[2,960]{1,0:T(2,128)S(1)} %pad_maximum_fusion.14), channel_id=1, replica_groups=mesh['ctx'=8,'wsh'=4] {'wsh','ctx'}, use_global_device_ids=true, to_apply=%region_23.25 | all-reduce | flops 1920 | bytes 15360 | tf_op jit(solution)/shard_map/psum | solution.py:438
  764.9 10.6 %all_gather.57 = bf16[8,240,120]{2,1,0:T(8,128)(2,1)S(1)} all-gather(bf16[1,240,120]{2,1,0:T(8,128)(2,1)} %reduce-scatter.18.cloned.1.call-done), channel_id=1, replica_groups=mesh['ctx'=8,'wsh'=4] {'ctx'}, dimensions={0}, use_global_device_ids=true | all-gather | bytes 518400 | tf_op jit(solution)/shard_map/all_gather | solution.py:429
  777.1 3.1 bitcast_convert_fusion
  780.2 3.2 copy.219
  783.4 3.4 reduce-scatter.14.cloned.1.call-done
  786.8 10.8 %all_gather.56 = bf16[8,240,200]{1,2,0:T(8,128)(2,1)S(1)} all-gather(bf16[1,240,200]{1,2,0:T(8,128)(2,1)} %reduce-scatter.14.cloned.1.call-done), channel_id=1, replica_groups=mesh['ctx'=8,'wsh'=4] {'ctx'}, dimensions={0}, use_global_device_ids=true | all-gather | bytes 864000 | tf_op jit(solution)/shard_map/all_gather | solution.py:429
  800.0 16.2 %all-gather.17.cloned.1.call-done = bf16[8,240,640]{2,1,0:T(8,128)(2,1)} async-done(((bf16[1,240,640]{2,1,0:T(8,128)(2,1)}), bf16[8,240,640]{2,1,0:T(8,128)(2,1)}) %all-gather.17.cloned.1.call-update) | async-done | bytes 2457616 | tf_op jit(solution)/shard_map/all_gather | solution.py:429
  816.2 2.0 convert_bitcast_fusion
  818.8 2.6 fusion.117
  (319 shorter events, 85.2 us)
Async XLA Ops:
  7.2 86.2 %copy-start = (bf16[640,960]{0,1:T(8,128)(2,1)S(1)}, bf16[640,960]{0,1:T(8,128)(2,1)}, u32[]{:S(2)}) copy-start(bf16[640,960]{0,1:T(8,128)(2,1)} %param.32) | copy-start | bytes 3686404
  7.2 66.9 %all-gather.27.cloned.1.call-start = ((), (), s32[]{:S(2)}) async-start(), calls=%async_computation.21 | async-start | bytes 3379200 | tf_op jit(solution)/shard_map/all_gather | solution.py:20
  9.5 4.0 copy-start.53
  9.5 4.0 copy-start.54
  9.5 16.8 %copy-start.50 = (s32[1024]{0:T(1024)S(1)}, s32[1024]{0:T(1024)}, u32[]{:S(2)}) copy-start(s32[1024]{0:T(1024)} %param.23) | copy-start | bytes 12292
  9.5 16.9 %copy-start.16 = (bf16[1,128,960]{1,2,0:T(8,128)(2,1)S(1)}, bf16[1,128,960]{1,2,0:T(8,128)(2,1)}, u32[]{:S(2)}) copy-start(bf16[1,128,960]{1,2,0:T(8,128)(2,1)} %param.22) | copy-start | bytes 737284
  11.7 120.6 %all-gather.21.cloned.1.call-start = ((), (), s32[]{:S(2)}) async-start(), calls=%async_computation.18 | async-start | bytes 2027520 | tf_op jit(solution)/shard_map/all_gather | solution.py:20
  13.4 144.8 %all-gather.15.cloned.1.call-start = ((), (), s32[]{:S(2)}) async-start(), calls=%async_computation.8 | async-start | bytes 1474560 | tf_op jit(solution)/shard_map/all_gather | solution.py:271
  26.6 61.1 %copy-start.48 = (f32[128]{0:T(128)}, f32[128]{0:T(128)S(1)}, u32[]{:S(2)}) copy-start(f32[128]{0:T(128)S(1)} %add_rsqrt_fusion.1) | copy-start | bytes 1540
  26.7 110.4 %copy-start.38 = (f32[128,32]{0,1:T(8,128)}, f32[128,32]{0,1:T(8,128)S(1)}, u32[]{:S(2)}) copy-start(f32[128,32]{0,1:T(8,128)S(1)} %get-tuple-element.656) | copy-start | bytes 49156
  26.7 110.4 %copy-start.40 = (f32[128,32]{0,1:T(8,128)}, f32[128,32]{0,1:T(8,128)S(1)}, u32[]{:S(2)}) copy-start(f32[128,32]{0,1:T(8,128)S(1)} %get-tuple-element.657) | copy-start | bytes 49156
  90.7 1.7 copy-start.28
  92.4 152.4 %all-gather.23.cloned.1.call-start = ((), (), s32[]{:S(2)}) async-start(), calls=%async_computation.19 | async-start | bytes 10137600 | tf_op jit(solution)/shard_map/all_gather | solution.py:20
  93.3 218.6 %all-gather.25.cloned.1.call-start = ((), (), s32[]{:S(2)}) async-start(), calls=%async_computation.20 | async-start | bytes 5406720 | tf_op jit(solution)/shard_map/all_gather | solution.py:20
  94.3 349.1 %all-reduce.3.cloned.1.call-start = ((), (), s32[]{:S(2)}) async-start(), calls=%async_computation.23 | async-start | bytes 10485760
  138.4 21.5 %copy-start.12 = (bf16[64,15,64]{0,2,1:T(8,128)(2,1)}, bf16[64,15,64]{0,2,1:T(8,128)(2,1)S(1)}, u32[]{:S(2)}) copy-start(bf16[64,15,64]{0,2,1:T(8,128)(2,1)S(1)} %get-tuple-element.645) | copy-start | bytes 368644
  138.4 21.5 %copy-start.14 = (bf16[64,15,64]{0,2,1:T(8,128)(2,1)}, bf16[64,15,64]{0,2,1:T(8,128)(2,1)S(1)}, u32[]{:S(2)}) copy-start(bf16[64,15,64]{0,2,1:T(8,128)(2,1)S(1)} %get-tuple-element.644) | copy-start | bytes 368644
  173.9 2.3 copy-start.35
  176.8 2.3 copy-start.35
  180.2 3.1 copy-start.5
  180.2 3.1 copy-start.6
  180.2 2.0 copy-start.8
  180.2 2.1 copy-start.17
  181.3 2.0 copy-start.23
  181.5 1.8 copy-start.25
  182.3 1.7 copy-start.34
  183.3 138.5 %copy-start.10 = (f32[128,960]{0,1:T(8,128)}, f32[128,960]{0,1:T(8,128)S(1)}, u32[]{:S(2)}) copy-start(f32[128,960]{0,1:T(8,128)S(1)} %get-tuple-element.663) | copy-start | bytes 1474564
  183.3 138.4 %copy-start.45 = (f32[128]{0:T(128)}, f32[128]{0:T(128)S(1)}, u32[]{:S(2)}) copy-start(f32[128]{0:T(128)S(1)} %add_rsqrt_fusion) | copy-start | bytes 1540
  264.3 47.6 %copy-start.27 = (bf16[1,128,960]{1,2,0:T(8,128)(2,1)S(1)}, bf16[1,128,960]{1,2,0:T(8,128)(2,1)}, u32[]{:S(2)}) copy-start(bf16[1,128,960]{1,2,0:T(8,128)(2,1)} %param.33) | copy-start | bytes 737284
  311.9 6.5 copy-start.2
  318.3 3.4 copy-start.29
  318.3 3.4 copy-start.31
  318.3 3.6 copy-start.9
  322.0 1.1 copy-start.24
  324.0 1.6 copy-start.15
  324.0 1.5 copy-start.44
  325.6 2.2 copy-start.43
  332.6 2.2 copy-start.43
  339.5 5.0 copy-start.3
  352.5 132.2 %reduce-scatter.26.cloned.1.call-start = ((), (), s32[]{:S(2)}) async-start(), calls=%async_computation.22 | async-start | bytes 1474560
  387.7 1.9 copy-start.52
  389.6 2.9 copy-start.32
  392.3 1.2 copy-start.30
  392.3 1.2 copy-start.46
  392.3 174.6 %reduce-scatter.20.cloned.1.call-start = ((), (), s32[]{:S(2)}) async-start(), calls=%async_computation.13 | async-start | bytes 11059200 | tf_op jit(solution)/shard_map/reduce_scatter | solution.py:24
  417.7 1.0 copy-start.20
  417.7 1.1 copy-start.26
  417.7 193.3 %reduce-scatter.16.cloned.1.call-start = ((), (), s32[]{:S(2)}) async-start(), calls=%async_computation.11 | async-start | bytes 2211840 | tf_op jit(solution)/shard_map/reduce_scatter | solution.py:24
  428.9 1.2 copy-start.4
  429.0 207.4 %reduce-scatter.24.cloned.1.call-start = ((), (), s32[]{:S(2)}) async-start(), calls=%async_computation.16 | async-start | bytes 819200 | tf_op jit(solution)/shard_map/reduce_scatter | solution.py:25
  430.4 15.8 %copy-start.39 = (f32[128,32]{0,1:T(8,128)S(1)}, f32[128,32]{0,1:T(8,128)}, u32[]{:S(2)}) copy-start(f32[128,32]{0,1:T(8,128)} %copy-done.38) | copy-start | bytes 49156
  430.4 15.8 %copy-start.41 = (f32[128,32]{0,1:T(8,128)S(1)}, f32[128,32]{0,1:T(8,128)}, u32[]{:S(2)}) copy-start(f32[128,32]{0,1:T(8,128)} %copy-done.40) | copy-start | bytes 49156
  446.1 239.1 %reduce-scatter.12.cloned.1.call-start = ((), (), s32[]{:S(2)}) async-start(), calls=%async_computation.9 | async-start | bytes 3686400 | tf_op jit(solution)/shard_map/reduce_scatter | solution.py:24
  446.2 39.8 %copy-start.18 = (bf16[1,128,960]{1,2,0:T(8,128)(2,1)S(1)}, bf16[1,128,960]{1,2,0:T(8,128)(2,1)}, u32[]{:S(2)}) copy-start(bf16[1,128,960]{1,2,0:T(8,128)(2,1)} %param.22) | copy-start | bytes 737284
  446.2 39.8 %copy-start.49 = (f32[128]{0:T(128)S(1)}, f32[128]{0:T(128)}, u32[]{:S(2)}) copy-start(f32[128]{0:T(128)} %copy-done.48) | copy-start | bytes 1540
  509.2 208.5 %copy-start.22 = (bf16[128,2560]{1,0:T(8,128)(2,1)S(1)}, bf16[128,2560]{1,0:T(8,128)(2,1)}, u32[]{:S(2)}) copy-start(bf16[128,2560]{1,0:T(8,128)(2,1)} %get-tuple-element.633) | copy-start | bytes 1966084
  509.2 208.4 %reduce-scatter.22.cloned.1.call-start = ((), (), s32[]{:S(2)}) async-start(), calls=%async_computation.14 | async-start | bytes 1536000 | tf_op jit(solution)/shard_map/reduce_scatter | solution.py:25
  566.9 198.0 %reduce-scatter.18.cloned.1.call-start = ((), (), s32[]{:S(2)}) async-start(), calls=%async_computation.12 | async-start | bytes 307200 | tf_op jit(solution)/shard_map/reduce_scatter | solution.py:25
  611.0 166.0 %all-gather.19.cloned.1.call-start = ((), (), s32[]{:S(2)}) async-start(), calls=%async_computation.17 | async-start | bytes 1474560 | tf_op jit(solution)/shard_map/all_gather | solution.py:429
  636.4 150.4 %reduce-scatter.14.cloned.1.call-start = ((), (), s32[]{:S(2)}) async-start(), calls=%async_computation.10 | async-start | bytes 512000 | tf_op jit(solution)/shard_map/reduce_scatter | solution.py:25
  685.2 130.9 %all-gather.17.cloned.1.call-start = ((), (), s32[]{:S(2)}) async-start(), calls=%async_computation.15 | async-start | bytes 2764800 | tf_op jit(solution)/shard_map/all_gather | solution.py:429
  717.7 5.0 copy-start.7
  722.7 1.5 copy-start.51
  818.8 2.6 copy-start.1
  (12 other events, 10.0 us)
Sparse Core Ops, SparseCore 0:
  11.8 62.2 all-gather.26
  77.6 54.6 all-gather.20
  134.7 23.3 all-gather.14
  161.5 83.1 all-gather.22
  248.0 63.8 all-gather.24
  352.6 90.8 all-reduce.2
  447.3 37.2 reduce-scatter.25
  488.2 78.6 reduce-scatter.19
  570.8 40.1 reduce-scatter.15
  613.7 22.5 reduce-scatter.23
  639.8 45.3 reduce-scatter.11
  687.4 30.2 reduce-scatter.21
  719.9 18.5 reduce-scatter.17
  740.3 23.1 all-gather.18
  765.6 21.1 reduce-scatter.13
  788.5 27.5 all-gather.16

commit v2 on v1

--- a/solution.py
+++ b/solution.py
@@ -213,30 +213,54 @@
     groups = lax.axis_size("wsh")
     spot = lax.axis_index("ctx")
 
-    def spread(shard, columns):
-        rows, width = shard.shape
-        if columns:
-            piece = lax.dynamic_slice_in_dim(shard, spot * (width // parts), width // parts, 1)
-        else:
-            piece = lax.dynamic_slice_in_dim(shard, spot * (rows // parts), rows // parts, 0)
-        pieces = gather_all(piece)
-        if columns:
-            return (
-                pieces.reshape(groups, parts, rows, width // parts)
-                .transpose(0, 2, 1, 3)
-                .reshape(groups * rows, width)
-            )
-        return pieces.reshape(groups * rows, width)
-
-    gains = lax.all_gather(jnp.stack([first_gain, second_gain]), "wsh", axis=0, tiled=False)
-    gains = gains.transpose(1, 0, 2).reshape(2, -1)
-    first_scale, second_scale = gains[0], gains[1]
-    first_matrices = spread(jnp.concatenate([query_weight, key_weight, value_proj_weight], axis=1), True)
+    def own_columns(shard):
+        width = shard.shape[1] // parts
+        return lax.dynamic_slice_in_dim(shard, spot * width, width, 1)
+
+    def joined(pieces):
+        rows, width = pieces.shape[1:]
+        return (
+            pieces.reshape(groups, parts, rows, width)
+            .transpose(0, 2, 1, 3)
+            .reshape(groups * rows, parts * width)
+        )
+
     query_width = query_weight.shape[1]
     key_width = key_weight.shape[1]
-    output_matrix = spread(output_weight, True)
-    wide_matrices = spread(jnp.concatenate([gate_weight, up_weight], axis=1), True)
-    down_matrix = spread(down_weight, False)
+    own_gain = first_gain.shape[0]
+    first_piece = own_columns(
+        jnp.concatenate([query_weight, key_weight, value_proj_weight], axis=1)
+    )
+    first_width = first_piece.shape[1]
+    gain_rows = -(-2 * own_gain // first_width)
+
+    def gain_block(pair):
+        lead = pair.shape[:-1]
+        pad = gain_rows * first_width - pair.shape[-1]
+        filled = jnp.concatenate([pair, jnp.zeros(lead + (pad,), pair.dtype)], axis=-1)
+        return filled.reshape(lead + (gain_rows, first_width))
+
+    first_pieces = gather_all(
+        jnp.concatenate(
+            [first_piece, gain_block(jnp.concatenate([first_gain, second_gain]))], axis=0
+        )
+    )
+    first_matrices = joined(first_pieces[:, :own_gain])
+    gains = first_pieces.reshape(groups, parts, own_gain + gain_rows, first_width)[:, 0, own_gain:]
+    gains = gains.reshape(groups, gain_rows * first_width)[:, : 2 * own_gain]
+    gains = gains.reshape(groups, 2, own_gain).transpose(1, 0, 2).reshape(2, groups * own_gain)
+    first_scale, second_scale = gains[0], gains[1]
+    wide_piece = own_columns(jnp.concatenate([gate_weight, up_weight], axis=1))
+    wide_width = wide_piece.shape[1]
+    wide_pieces = gather_all(
+        jnp.concatenate([wide_piece, own_columns(output_weight)], axis=1)
+    )
+    wide_matrices = joined(wide_pieces[..., :wide_width])
+    output_matrix = joined(wide_pieces[..., wide_width:])
+    down_rows = down_weight.shape[0] // parts
+    down_matrix = gather_all(
+        lax.dynamic_slice_in_dim(down_weight, spot * down_rows, down_rows, 0)
+    ).reshape(groups * down_weight.shape[0], down_weight.shape[1])
     hidden_units = gate_weight.shape[1]
     tokens = layer_input[0]
     incoming_rows = cotangent[0]
@@ -346,6 +370,36 @@
     )
     mixed_low = mixed_back.astype(jnp.bfloat16)
     attention_result_back = times_transposed(mixed_low, output_matrix).astype(jnp.bfloat16)
+
+    def cut(gradient):
+        rows, width = gradient.shape
+        return (
+            gradient.astype(jnp.bfloat16)
+            .reshape(groups, rows // groups, parts, width // parts)
+            .transpose(2, 0, 1, 3)
+        )
+
+    splits = own_gain // down_rows
+    down_width = down_weight.shape[1] // splits
+    down_blocks = [
+        token_sum(activated, incoming_rows[:, index * down_width : (index + 1) * down_width])
+        .astype(jnp.bfloat16)
+        .reshape(groups, parts, down_rows, down_width)
+        .transpose(1, 0, 2, 3)
+        for index in range(splits)
+    ]
+    wide_sent = jnp.concatenate(
+        [
+            cut(token_sum(hidden_two, wide_back)),
+            jnp.concatenate(down_blocks, axis=2),
+            cut(token_sum(attention_result, mixed_low)),
+        ],
+        axis=-1,
+    )
+    wide_sent, attention_result_back = lax.optimization_barrier(
+        (wide_sent, attention_result_back)
+    )
+    wide_near = lax.psum_scatter(wide_sent, "ctx", scatter_dimension=0, tiled=False)
     backward_groups = attention_result_back.reshape(
         worker_rows, KEY_VALUE_HEADS, head_groups, HEAD_SIZE
     )
@@ -379,6 +433,9 @@
         query_parts.append(query_half)
     query_gradient_back = jnp.concatenate(query_parts, axis=0).reshape(
         worker_rows, QUERY_HEADS, HEAD_SIZE
+    )
+    wide_near, keys_gradient_back, values_gradient_back = lax.optimization_barrier(
+        (wide_near, keys_gradient_back, values_gradient_back)
     )
     both_share = lax.psum_scatter(
         blocks_per_worker(
@@ -418,26 +475,35 @@
         first_back, normed_one, scale_one, first_scale.astype(jnp.float32)
     )
 
-    def collect(gradient, columns):
-        rows, width = gradient.shape
-        own_rows = rows // groups
-        sent = gradient.astype(jnp.bfloat16)
-        if columns:
-            sent = sent.reshape(groups, own_rows, parts, width // parts).transpose(2, 0, 1, 3)
-        else:
-            sent = sent.reshape(groups, parts, own_rows // parts, width).transpose(1, 0, 2, 3)
-        pieces = lax.all_gather(scatter_all(sent), "ctx", axis=0, tiled=False)
-        if columns:
-            pieces = pieces.transpose(1, 0, 2)
-        return pieces.reshape(own_rows, width).astype(jnp.float32)
-
-    down_total = collect(token_sum(activated, incoming_rows), False)
-    wide_total = collect(token_sum(hidden_two, wide_back), True)
-    output_total = collect(token_sum(attention_result, mixed_low), True)
-    first_total = collect(token_sum(hidden_first, first_cols), True)
-    gain_sums = lax.psum(jnp.stack([first_gradient, second_gradient]), ("wsh", "ctx"))
-    own_gain = first_gain.shape[0]
-    gain_sums = lax.dynamic_slice_in_dim(gain_sums, lax.axis_index("wsh") * own_gain, own_gain, 1)
+    def own_rows_of(pieces):
+        count, rows, width = pieces.shape
+        return pieces.transpose(1, 0, 2).reshape(rows, count * width).astype(jnp.float32)
+
+    wide_share = lax.psum_scatter(wide_near, "wsh", scatter_dimension=0, tiled=False)
+    wide_total = lax.all_gather(wide_share, "ctx", axis=0, tiled=False)
+    output_total = own_rows_of(wide_total[..., wide_width + down_width :])
+    down_total = (
+        wide_total[..., wide_width : wide_width + down_width]
+        .reshape(parts, splits, down_rows, down_width)
+        .transpose(0, 2, 1, 3)
+        .reshape(down_weight.shape)
+        .astype(jnp.float32)
+    )
+    wide_total = own_rows_of(wide_total[..., :wide_width])
+    gain_pair = jnp.stack([first_gradient, second_gradient]).astype(jnp.bfloat16)
+    gain_pair = gain_pair.reshape(2, groups, own_gain).transpose(1, 0, 2)
+    gain_pair = gain_block(gain_pair.reshape(groups, 2 * own_gain))
+    first_sent = jnp.concatenate(
+        [
+            cut(token_sum(hidden_first, first_cols)),
+            jnp.broadcast_to(gain_pair[None], (parts,) + gain_pair.shape),
+        ],
+        axis=2,
+    )
+    first_total = lax.all_gather(scatter_all(first_sent), "ctx", axis=0, tiled=False)
+    gain_sums = first_total[0, own_gain:].reshape(gain_rows * first_width)[: 2 * own_gain]
+    gain_sums = gain_sums.reshape(2, own_gain).astype(jnp.float32)
+    first_total = own_rows_of(first_total[:, :own_gain])
     return (
         layer_output[None],
         input_back[None],

time: 840 us -> 780 us (0.929)
  blocking collectives: 73.1 us -> 11.1 us
  waiting for transfers between devices: 479 us -> 420 us
  local copies, waits for them, and re-layouts: 149 us -> 186 us
  matrix products: 77.9 us -> 95.9 us
    reduce_scatter x0 -> x2, waiting for transfers between devices: none -> 125 us  [the longest x1 77.1 us: per_device(): lax.psum_scatter(wide_sent, 'ctx', scatter_dimension=0, tiled=False)]
    reduce_scatter x3 -> x1, waiting for transfers between devices: 150 us -> 46 us  [scatter_all(): near = lax.psum_scatter(pieces, 'ctx', scatter_dimension=0, tiled=False)]
    reduce_scatter x4 -> x1, waiting for transfers between devices: 60.8 us -> 16.6 us  [scatter_all(): return lax.psum_scatter(near, 'wsh', scatter_dimension=0, tiled=False)]
    psum x1 -> x0, blocking collectives: 39 us -> none  [per_device(): lax.psum(jnp.stack([first_gradient, second_gradient]), ('wsh', 'ctx'))]
    concatenate x1 -> x4, local copies, waits for them, and re-layouts: 1.28 us -> 30 us  [the longest x1 24.7 us: per_device(): jnp.concatenate([cut(token_sum(hidden_two, wide_back)), jnp.concatenate(d...]
    all_gather x4 -> x3, waiting for transfers between devices: 180 us -> 157 us  [gather_all(): return lax.all_gather(piece, ('wsh', 'ctx'), axis=0, tiled=False)]
    all_gather x3 -> x1, blocking collectives: 34.1 us -> 11.1 us  [per_device(): lax.all_gather(scatter_all(first_sent), 'ctx', axis=0, tiled=False)]
    slice x0 -> x9, local copies, waits for them, and re-layouts: none -> 15.3 us  [the longest x1 8.32 us: per_device(): wide_matrices = joined(wide_pieces[..., :wide_width])]
  transfers between devices with their start and end apart: 16 -> 10, of which waited for: 14 -> 10; matrix products, arithmetic and copies ran while one was open for 24% -> 16% of each run, Pallas kernels for 0% -> 0%
where the time goes in v2:
time: 780 us; the launch traced here: 768 us
  waiting for transfers between devices  420 us (54%)
  local copies, waits for them, and re-layouts  186 us (24%)
  matrix products  95.9 us (12%)
  other arithmetic  37.1 us (5%)
  between operations  16.9 us (2%)
  blocking collectives  11.1 us (1%)
    all_gather x3, waiting for transfers between devices, gather_all(): return lax.all_gather(piece, ('wsh', 'ctx'), axis=0, tiled=False)  157 us
    reduce_scatter x1, waiting for transfers between devices, per_device(): lax.psum_scatter(wide_sent, 'ctx', scatter_dimension=0, tiled=False)  77.1 us
    reduce_scatter x1, waiting for transfers between devices, per_device(): lax.psum_scatter(wide_near, 'wsh', scatter_dimension=0, tiled=False)  47.9 us
    reduce_scatter x1, waiting for transfers between devices, scatter_all(): near = lax.psum_scatter(pieces, 'ctx', scatter_dimension=0, tiled=False)  46 us
    unnamed x11, waiting for transfers between devices  37.5 us
    reshape x5, local copies, waits for them, and re-layouts, cut(): return gradient.astype(jnp.bfloat16).reshape(groups, rows // groups, part...  29.4 us
    unnamed x102, local copies, waits for them, and re-layouts  28 us
    dot_general x6, matrix products, token_sum(): lax.dot_general(left, right, (((0,), (0,)), ((), ())), preferred_element_...  27.3 us
  transfers between devices with their start and end apart: 10, of which 10 were waited for; matrix products, arithmetic and copies ran while one was open for 16% of the time, Pallas kernels for 0%

profile of v2, /device:TPU:0, one launch (start us, length us, event | category | flops | bytes accessed | tf_op | source)
XLA Modules:
  0.0 768.1 jit_solution(6255780006247691493)
XLA Ops:
  12.2 61.6 %all-gather.18.cloned.1.call-done = bf16[32,243,200]{1,2,0:T(8,128)(2,1)} async-done(((bf16[1,243,200]{1,2,0:T(8,128)(2,1)}), bf16[32,243,200]{1,2,0:T(8,128)(2,1)}) %all-gather.18.cloned.1.call-update) | async-done | bytes 3110416 | tf_op jit(solution)/shard_map/all_gather | solution.py:20
  73.8 6.2 copy.326
  80.0 7.4 reshape.435
  90.1 3.0 fusion.94
  102.6 14.8 %all-gather.10.cloned.1.call-done = bf16[1024,640]{0,1:T(8,128)(2,1)} async-done(((bf16[128,640]{0,1:T(8,128)(2,1)}), bf16[1024,640]{0,1:T(8,128)(2,1)}) %all-gather.10.cloned.1.call-update) | async-done | bytes 1310736 | tf_op jit(solution)/shard_map/all_gather | solution.py:295
  119.1 1.8 gather_fusion.1
  123.4 8.4 %while.57 = (s32[]{:T(128)}, f32[64,5,3]{0,2,1:T(4,128)S(1)}, f32[64,5,3]{0,2,1:T(4,128)S(1)}, f32[64,5,3,64]{0,3,2,1:T(8,128)S(1)}, s32[]{:T(128)}, /*index=5*/...) while((s32[]{:T(128)}, f32[64,5,3]{0,2,1:T(4,128)S(1)}, ...), condition=%wide.region_11.13_spmd, body=%wide.region_8.12_spmd.sunk | while | flops 64776068 | bytes 4370375 | solution.py:123
  133.1 4.8 while.56
  139.0 73.6 %all-gather.14.cloned.1.call-done = bf16[7680,760]{1,0:T(8,128)(2,1)} async-done(((bf16[240,760]{1,0:T(8,128)(2,1)}), bf16[7680,760]{1,0:T(8,128)(2,1)}) %all-gather.14.cloned.1.call-update) | async-done | bytes 11673616 | tf_op jit(solution)/shard_map/all_gather | solution.py:20
  212.6 2.9 slice.245
  215.6 8.3 %slice.247 = bf16[32,240,640]{2,1,0:T(8,128)(2,1)} slice(bf16[32,240,760]{2,1,0:T(8,128)(2,1)} %bitcast.406), slice={[0:32], [0:240], [0:640]} | slice | bytes 19660800 | tf_op jit(solution)/shard_map/slice | solution.py:258
  223.9 3.3 copy.271
  227.2 3.4 reshape.444
  230.6 9.6 %copy.272 = bf16[4,240,8,640]{3,2,1,0:T(8,128)(2,1)} copy(bf16[4,240,8,640]{3,1,2,0:T(8,128)(2,1)} %bitcast.390) | data formatting | bytes 19660800 | tf_op jit(solution)/shard_map/transpose | solution.py:224
  240.2 10.0 %copy.320 = bf16[120,8,8,640]{3,1,2,0:T(8,128)(2,1)} copy(bf16[120,8,8,640]{3,2,1,0:T(8,128)(2,1)} %bitcast.391) | data formatting | bytes 19660800
  251.1 7.2 fusion.117
  258.3 21.6 %all-gather.16.cloned.1.call-done = bf16[2560,960]{1,0:T(8,128)(2,1)} async-done(((bf16[80,960]{1,0:T(8,128)(2,1)}), bf16[2560,960]{1,0:T(8,128)(2,1)}) %all-gather.16.cloned.1.call-update) | async-done | bytes 4915216 | tf_op jit(solution)/shard_map/all_gather | solution.py:20
  279.8 5.5 multiply_convert_fusion.1
  285.3 7.4 multiply_reduce_fusion
  292.7 17.4 %convolution_convert_fusion = bf16[960,5120]{1,0:T(8,128)(2,1)} fusion(bf16[128,2560]{1,0:T(8,128)(2,1)S(1)} %get-tuple-element.673, bf16[128,2560]{1,0:T(8,128)(2,1)S(1)} %get-tuple-element.672, f32[128,960]{0,1:T(8,128)S(1)} %get-tuple-element.704, f32[960]{0:T(1024)S(1)} %reshape.461, f32[128]{0:T(128)S(1)} %add_rsqrt_fusion), kind=kOutput, calls=%fused_computation.98 | convolution fusion | flops 1266196480 | bytes 11636992 | tf_op jit(solution)/shard_map/dot_general | solution.py:39
  310.1 1.7 convolution_convert_fusion.1
  311.8 1.7 convolution_convert_fusion.2
  313.6 1.7 convolution_convert_fusion.3
  315.6 2.0 convolution_convert_fusion.5
  318.2 9.9 %copy.321 = bf16[120,8,8,640]{3,2,1,0:T(8,128)(2,1)} copy(bf16[120,8,8,640]{3,1,2,0:T(8,128)(2,1)} %bitcast.388) | data formatting | bytes 19660800
  328.2 8.9 %copy.325 = bf16[4,240,8,640]{3,1,0,2:T(8,128)(2,1)} copy(bf16[4,240,8,640]{3,2,1,0:T(8,128)(2,1)} %bitcast.392) | data formatting | bytes 19660800 | tf_op jit(solution)/shard_map/reshape | solution.py:378
  337.1 3.6 copy.278
  340.7 3.8 copy.277
  344.5 3.8 copy.276
  348.4 3.4 pad_maximum_fusion
  351.7 3.2 copy.280
  354.9 3.2 reshape.452
  358.1 1.8 copy.327
  359.9 24.7 %concatenate.80 = bf16[8,4,240,1080]{3,2,1,0:T(8,128)(2,1)} concatenate(bf16[8,4,240,640]{3,2,1,0:T(8,128)(2,1)} %bitcast.389, bf16[8,4,240,320]{3,2,1,0:T(8,128)(2,1)} %copy.280, bf16[8,4,240,120]{3,2,1,0:T(8,128)(2,1)S(1)} %bitcast.410), dimensions={3} | concatenate | bytes 33177600 | tf_op jit(solution)/shard_map/concatenate | solution.py:391
  388.5 14.8 %while.58 = (s32[]{:T(128)}, f32[64,5,3,64]{0,3,2,1:T(8,128)S(1)}, f32[1024,5,64]{0,2,1:T(8,128)S(1)}, f32[1024,5,64]{0,2,1:T(8,128)}, s32[]{:T(128)}, /*index=5...) while((s32[]{:T(128)}, f32[64,5,3,64]{0,3,2,1:T(8,128)S(1)}, ...), condition=%wide.region_16.18_spmd, body=%wide.region_15.17_spmd.sunk | while | flops 159494144 | bytes 7996679 | solution.py:195
  393.7 2.0 fusion.225
  401.2 2.0 fusion.225
  404.1 22.9 %while.59 = (s32[]{:T(128)}, f32[64,5,3,64]{0,3,2,1:T(8,128)S(1)}, f32[1024,5,64]{0,2,1:T(8,128)S(1)}, f32[1024,5,64]{0,2,1:T(8,128)}, s32[]{:T(128)}, /*index=5...) while((s32[]{:T(128)}, f32[64,5,3,64]{0,3,2,1:T(8,128)S(1)}, ...), condition=%wide.region_18.20_spmd, body=%wide.region_17.19_spmd.sunk | while | flops 159494144 | bytes 7382251 | solution.py:195
  409.8 2.0 fusion.240
  417.4 2.0 fusion.240
  425.0 2.0 fusion.240
  427.0 77.1 %reduce-scatter.8.cloned.1.call-done = bf16[1,4,240,1080]{3,2,1,0:T(8,128)(2,1)} async-done(((bf16[8,4,240,1080]{3,2,1,0:T(8,128)(2,1)}), bf16[1,4,240,1080]{3,2,1,0:T(8,128)(2,1)}) %reduce-scatter.8.cloned.1.call-update) | async-done | bytes 2073616 | tf_op jit(solution)/shard_map/reduce_scatter | solution.py:402
  505.4 1.9 concatenate.84
  507.3 1.9 copy.282
  510.1 1.9 concatenate.83
  515.4 1.8 gather_fusion.2
  517.2 2.6 broadcast_select_fusion
  520.7 36.6 %reduce-scatter.16.cloned.1.call-done = bf16[128,640]{1,0:T(8,128)(2,1)} async-done(((bf16[1024,640]{1,0:T(8,128)(2,1)}), bf16[128,640]{1,0:T(8,128)(2,1)}) %reduce-scatter.16.cloned.1.call-update) | async-done | bytes 163856
  558.7 3.4 fusion.87
  562.1 2.7 convolution_convert_fusion.4
  565.4 9.2 %reshape.521 = bf16[4,240,8,200]{3,2,1,0:T(8,128)(2,1)} reshape(bf16[960,1600]{1,0:T(8,128)(2,1)} %convolution_convert_fusion.4) | data formatting | bytes 6144000 | tf_op jit(solution)/shard_map/reshape | solution.py:378
  574.6 6.3 copy.311
  581.3 4.9 pad_maximum_fusion.1
  586.1 2.1 copy.287
  589.1 46.0 %reduce-scatter.10.cloned.1.call-done = bf16[1,4,243,200]{2,3,1,0:T(8,128)(2,1)} async-done(((bf16[8,4,243,200]{2,3,1,0:T(8,128)(2,1)}), bf16[1,4,243,200]{2,3,1,0:T(8,128)(2,1)}) %reduce-scatter.10.cloned.1.call-update) | async-done | bytes 388816 | tf_op jit(solution)/shard_map/reduce_scatter | solution.py:24
  635.2 47.9 %reduce-scatter.14.cloned.1.call-done = bf16[1,240,1080]{2,1,0:T(8,128)(2,1)} async-done(((bf16[4,240,1080]{2,1,0:T(8,128)(2,1)}), bf16[1,240,1080]{2,1,0:T(8,128)(2,1)}) %reduce-scatter.14.cloned.1.call-update) | async-done | bytes 518416 | tf_op jit(solution)/shard_map/reduce_scatter | solution.py:482
  683.1 4.9 fusion.73
  689.0 16.6 %reduce-scatter.12.cloned.1.call-done = bf16[1,243,200]{1,2,0:T(8,128)(2,1)} async-done(((bf16[4,243,200]{1,2,0:T(8,128)(2,1)}), bf16[1,243,200]{1,2,0:T(8,128)(2,1)}) %reduce-scatter.12.cloned.1.call-update) | async-done | bytes 97216 | tf_op jit(solution)/shard_map/reduce_scatter | solution.py:25
  705.6 11.1 %all_gather.34 = bf16[8,243,200]{1,2,0:T(8,128)(2,1)S(1)} all-gather(bf16[1,243,200]{1,2,0:T(8,128)(2,1)} %reduce-scatter.12.cloned.1.call-done), channel_id=1, replica_groups=mesh['ctx'=8,'wsh'=4] {'ctx'}, dimensions={0}, use_global_device_ids=true | all-gather | bytes 874800 | tf_op jit(solution)/shard_map/all_gather | solution.py:503
  720.0 23.3 %all-gather.12.cloned.1.call-done = bf16[8,240,1080]{2,1,0:T(8,128)(2,1)} async-done(((bf16[1,240,1080]{2,1,0:T(8,128)(2,1)}), bf16[8,240,1080]{2,1,0:T(8,128)(2,1)}) %all-gather.12.cloned.1.call-update) | async-done | bytes 4147216 | tf_op jit(solution)/shard_map/all_gather | solution.py:483
  746.3 2.0 convert_bitcast_fusion
  748.9 2.6 fusion.121
  752.9 2.9 copy.291
  755.8 5.0 reshape.468
  (311 shorter events, 87.3 us)
Async XLA Ops:
  7.2 88.9 %copy-start = (bf16[640,960]{0,1:T(8,128)(2,1)S(1)}, bf16[640,960]{0,1:T(8,128)(2,1)}, u32[]{:S(2)}) copy-start(bf16[640,960]{0,1:T(8,128)(2,1)} %param.32) | copy-start | bytes 3686404
  7.2 4.7 copy-start.14
  7.2 66.6 %all-gather.18.cloned.1.call-start = ((), (), s32[]{:S(2)}) async-start(), calls=%async_computation.13 | async-start | bytes 3379200 | tf_op jit(solution)/shard_map/all_gather | solution.py:20
  10.6 106.8 %all-gather.10.cloned.1.call-start = ((), (), s32[]{:S(2)}) async-start(), calls=%async_computation.5 | async-start | bytes 1474560 | tf_op jit(solution)/shard_map/all_gather | solution.py:295
  12.1 77.4 %copy-start.41 = (f32[128]{0:T(128)}, f32[128]{0:T(128)S(1)}, u32[]{:S(2)}) copy-start(f32[128]{0:T(128)S(1)} %add_rsqrt_fusion.1) | copy-start | bytes 1540
  12.2 89.7 %copy-start.33 = (f32[128,32]{0,1:T(8,128)}, f32[128,32]{0,1:T(8,128)S(1)}, u32[]{:S(2)}) copy-start(f32[128,32]{0,1:T(8,128)S(1)} %get-tuple-element.697) | copy-start | bytes 49156
  12.2 89.7 %copy-start.35 = (f32[128,32]{0,1:T(8,128)}, f32[128,32]{0,1:T(8,128)S(1)}, u32[]{:S(2)}) copy-start(f32[128,32]{0,1:T(8,128)S(1)} %get-tuple-element.698) | copy-start | bytes 49156
  89.5 0.6 copy-start.37
  93.1 1.9 copy-start.26
  93.9 118.7 %all-gather.14.cloned.1.call-start = ((), (), s32[]{:S(2)}) async-start(), calls=%async_computation.11 | async-start | bytes 12165120 | tf_op jit(solution)/shard_map/all_gather | solution.py:20
  95.2 1.9 copy-start.44
  95.2 3.8 copy-start.43
  96.0 183.9 %all-gather.16.cloned.1.call-start = ((), (), s32[]{:S(2)}) async-start(), calls=%async_computation.12 | async-start | bytes 5406720 | tf_op jit(solution)/shard_map/all_gather | solution.py:20
  97.0 5.5 copy-start.40
  97.0 407.0 %reduce-scatter.8.cloned.1.call-start = ((), (), s32[]{:S(2)}) async-start(), calls=%async_computation.6 | async-start | bytes 19906560 | tf_op jit(solution)/shard_map/reduce_scatter | solution.py:402
  99.7 0.8 copy-start.47
  102.1 18.7 %copy-start.8 = (bf16[64,15,64]{0,2,1:T(8,128)(2,1)}, bf16[64,15,64]{0,2,1:T(8,128)(2,1)S(1)}, u32[]{:S(2)}) copy-start(bf16[64,15,64]{0,2,1:T(8,128)(2,1)S(1)} %get-tuple-element.686) | copy-start | bytes 368644
  102.2 18.7 %copy-start.10 = (bf16[64,15,64]{0,2,1:T(8,128)(2,1)}, bf16[64,15,64]{0,2,1:T(8,128)(2,1)S(1)}, u32[]{:S(2)}) copy-start(bf16[64,15,64]{0,2,1:T(8,128)(2,1)S(1)} %get-tuple-element.685) | copy-start | bytes 368644
  123.4 9.7 %copy-start.39 = (s32[64]{0:T(128)S(1)}, s32[64]{0:T(128)}, u32[]{:S(2)}) copy-start(s32[64]{0:T(128)} %get-tuple-element.1100) | copy-start | bytes 772
  131.9 0.6 copy-start.28
  133.1 1.6 copy-start.30
  134.8 0.6 copy-start.31
  135.4 1.6 copy-start.30
  137.1 0.6 copy-start.31
  137.9 77.7 %copy-start.4 = (bf16[1024,5,64]{0,2,1:T(8,128)(2,1)}, bf16[1024,5,64]{0,2,1:T(8,128)(2,1)S(1)}, u32[]{:S(2)}) copy-start(bf16[1024,5,64]{0,2,1:T(8,128)(2,1)S(1)} %get-tuple-element.1208) | copy-start | bytes 1966084
  137.9 77.6 %copy-start.5 = (bf16[1024,5,64]{0,2,1:T(8,128)(2,1)}, bf16[1024,5,64]{0,2,1:T(8,128)(2,1)S(1)}, u32[]{:S(2)}) copy-start(bf16[1024,5,64]{0,2,1:T(8,128)(2,1)S(1)} %get-tuple-element.1211) | copy-start | bytes 1966084
  138.9 76.7 %copy-start.20 = (bf16[64,5,3,64]{0,3,2,1:T(8,128)(2,1)}, bf16[64,5,3,64]{0,3,2,1:T(8,128)(2,1)S(1)}, u32[]{:S(2)}) copy-start(bf16[64,5,3,64]{0,3,2,1:T(8,128)(2,1)S(1)} %get-tuple-element.707) | copy-start | bytes 368644
  138.9 76.7 %copy-start.22 = (bf16[64,5,3,64]{0,3,2,1:T(8,128)(2,1)}, bf16[64,5,3,64]{0,3,2,1:T(8,128)(2,1)S(1)}, u32[]{:S(2)}) copy-start(bf16[64,5,3,64]{0,3,2,1:T(8,128)(2,1)S(1)} %get-tuple-element.708) | copy-start | bytes 368644
  139.0 111.1 %copy-start.24 = (bf16[128,5,3,64]{0,3,2,1:T(8,128)(2,1)}, bf16[128,5,3,64]{0,3,2,1:T(8,128)(2,1)S(1)}, u32[]{:S(2)}) copy-start(bf16[128,5,3,64]{0,3,2,1:T(8,128)(2,1)S(1)} %pad_maximum_fusion.10) | copy-start | bytes 737284
  240.2 10.0 %copy-start.15 = (bf16[1,128,960]{1,2,0:T(8,128)(2,1)S(1)}, bf16[1,128,960]{1,2,0:T(8,128)(2,1)}, u32[]{:S(2)}) copy-start(bf16[1,128,960]{1,2,0:T(8,128)(2,1)} %param.22) | copy-start | bytes 737284
  251.1 64.3 %copy-start.6 = (f32[128,960]{0,1:T(8,128)}, f32[128,960]{0,1:T(8,128)S(1)}, u32[]{:S(2)}) copy-start(f32[128,960]{0,1:T(8,128)S(1)} %get-tuple-element.704) | copy-start | bytes 1474564
  251.1 28.8 %copy-start.27 = (bf16[1,128,960]{1,2,0:T(8,128)(2,1)S(1)}, bf16[1,128,960]{1,2,0:T(8,128)(2,1)}, u32[]{:S(2)}) copy-start(bf16[1,128,960]{1,2,0:T(8,128)(2,1)} %param.33) | copy-start | bytes 737284
  285.3 28.3 %copy-start.12 = (bf16[128,2560]{1,0:T(8,128)(2,1)}, bf16[128,2560]{1,0:T(8,128)(2,1)S(1)}, u32[]{:S(2)}) copy-start(bf16[128,2560]{1,0:T(8,128)(2,1)S(1)} %get-tuple-element.674) | copy-start | bytes 1966084
  313.6 2.0 copy-start.25
  315.6 2.6 copy-start.18
  351.7 3.2 copy-start.17
  384.7 0.6 copy-start.48
  384.7 0.7 copy-start.32
  384.7 1.3 copy-start.29
  384.7 1.9 copy-start.21
  384.7 1.9 copy-start.23
  384.7 172.5 %reduce-scatter.16.cloned.1.call-start = ((), (), s32[]{:S(2)}) async-start(), calls=%async_computation.14 | async-start | bytes 1474560
  388.4 15.6 %copy-start.9 = (bf16[64,15,64]{0,2,1:T(8,128)(2,1)S(1)}, bf16[64,15,64]{0,2,1:T(8,128)(2,1)}, u32[]{:S(2)}) copy-start(bf16[64,15,64]{0,2,1:T(8,128)(2,1)} %copy-done.8) | copy-start | bytes 368644
  390.8 2.6 copy-start.11
  398.2 2.7 copy-start.11
  403.2 0.8 copy-start.2
  515.4 1.8 copy-start.46
  517.2 2.9 copy-start.45
  517.2 3.0 copy-start.3
  519.8 0.7 copy-start.34
  519.8 0.7 copy-start.36
  519.9 115.3 %reduce-scatter.10.cloned.1.call-start = ((), (), s32[]{:S(2)}) async-start(), calls=%async_computation.7 | async-start | bytes 3686400 | tf_op jit(solution)/shard_map/reduce_scatter | solution.py:24
  520.2 38.4 %copy-start.16 = (bf16[1,128,960]{1,2,0:T(8,128)(2,1)S(1)}, bf16[1,128,960]{1,2,0:T(8,128)(2,1)}, u32[]{:S(2)}) copy-start(bf16[1,128,960]{1,2,0:T(8,128)(2,1)} %param.22) | copy-start | bytes 737284
  520.2 38.4 %copy-start.38 = (f32[960]{0:T(1024)S(1)}, f32[960]{0:T(1024)}, u32[]{:S(2)}) copy-start(f32[960]{0:T(1024)} %copy-done.37) | copy-start | bytes 11524
  520.2 38.4 %copy-start.42 = (f32[128]{0:T(128)S(1)}, f32[128]{0:T(128)}, u32[]{:S(2)}) copy-start(f32[128]{0:T(128)} %copy-done.41) | copy-start | bytes 1540
  588.3 94.8 %copy-start.7 = (f32[128,960]{0,1:T(8,128)S(1)}, f32[128,960]{0,1:T(8,128)}, u32[]{:S(2)}) copy-start(f32[128,960]{0,1:T(8,128)} %copy-done.6) | copy-start | bytes 1474564
  588.3 94.8 %copy-start.13 = (bf16[128,2560]{1,0:T(8,128)(2,1)S(1)}, bf16[128,2560]{1,0:T(8,128)(2,1)}, u32[]{:S(2)}) copy-start(bf16[128,2560]{1,0:T(8,128)(2,1)} %copy-done.12) | copy-start | bytes 1966084
  588.3 94.8 %reduce-scatter.14.cloned.1.call-start = ((), (), s32[]{:S(2)}) async-start(), calls=%async_computation.9 | async-start | bytes 2764800 | tf_op jit(solution)/shard_map/reduce_scatter | solution.py:482
  589.0 116.6 %reduce-scatter.12.cloned.1.call-start = ((), (), s32[]{:S(2)}) async-start(), calls=%async_computation.8 | async-start | bytes 512000 | tf_op jit(solution)/shard_map/reduce_scatter | solution.py:25
  635.2 108.1 %all-gather.12.cloned.1.call-start = ((), (), s32[]{:S(2)}) async-start(), calls=%async_computation.10 | async-start | bytes 4976640 | tf_op jit(solution)/shard_map/all_gather | solution.py:483
  683.1 4.9 copy-start.19
  751.5 1.4 slice-start
  755.8 5.0 copy-start.1
Sparse Core Ops, SparseCore 0:
  11.4 62.3 all-gather.17
  94.1 23.2 all-gather.9
  120.9 91.6 all-gather.13
  215.9 63.9 all-gather.15
  384.9 119.1 reduce-scatter.7
  520.0 37.2 reduce-scatter.15
  588.4 46.7 reduce-scatter.9
  637.4 45.5 reduce-scatter.13
  685.3 20.2 reduce-scatter.11
  707.4 35.8 all-gather.11
